TPU v7x, 32 devices: a whole 2x2x4 slice. The times are simulated.
32 devices in a mesh: lat: 8 (over z, y), lay: 4 (over x, core).
Axes of the slice: x: 2, y: 2, z: 4, core: 2. Of those that a mesh axis runs over, the one named last changes fastest.
Arguments:
- wave_field: float32 [2, 32, 512, 512], P(None, 'lay', 'lat'), may hold values from -6 to 6
- contrast: float32 [32, 512, 512], P('lay', 'lat'), may hold values from 0.1 to 1.5
- layer_of_plane: int32 [32], replicated, may hold values from 0 to 7, never falling along the last dimension, each value on 1 to 8 neighbouring positions
- toeplitz_table: float32 [2, 8, 63], replicated, may hold values from -1 to 1
- hankel_table: float32 [2, 8, 63], replicated, may hold values from -1 to 1
- layer_rates: float32 [8], replicated, may hold values from 0.5 to 1.5
Outputs:
- scattered_field: float32 [2, 32, 512, 512], P(None, 'lay', 'lat')
Inputs may be any that keep to these rules, and one draw needn't show every extreme that they name: `layer_of_plane`: layer numbers never fall from one plane to the next; every layer holds 1 to 8 planes.
All inputs are finite; a program needn't handle non-finite values.
Results may differ from a plain program's by a relative error of at most 0.00007.
Values sent between devices are 32-bit elements; how exact they have to be, the bound alone decides.
A program may use at most 128 MiB of HBM per device.

v0:
```python
import math

import functools

import jax
import jax.numpy as jnp
import numpy as np
from jax import lax
from jax.experimental import pallas as pl
from jax.experimental.pallas import tpu as pltpu
from jax.sharding import PartitionSpec as P

HIGHEST = lax.Precision.HIGHEST


def signed_of(index, amount):
    return jnp.where(index >= amount // 2, index - amount, index).astype(jnp.float32) / (amount / 2)


def phase_tables(rows, cols, amount, sign):
    index_row = lax.broadcasted_iota(jnp.int32, (rows, cols), 0)
    index_col = lax.broadcasted_iota(jnp.int32, (rows, cols), 1)
    angle = 2.0 * math.pi / amount * (index_row * index_col % amount).astype(jnp.float32)
    return (jnp.cos(angle), sign * jnp.sin(angle))


def complex_apply(real_part, imag_part, cos_table, sin_table, form):
    out_real = jnp.einsum(form, real_part, cos_table, precision=HIGHEST) - jnp.einsum(
        form, imag_part, sin_table, precision=HIGHEST
    )
    out_imag = jnp.einsum(form, real_part, sin_table, precision=HIGHEST) + jnp.einsum(
        form, imag_part, cos_table, precision=HIGHEST
    )
    return (out_real, out_imag)


def fourier_last(real_part, imag_part, sign, factor):
    amount = real_part.shape[-1]
    leading = real_part.shape[:-1]
    first = 1
    for divisor in range(1, math.isqrt(amount) + 1):
        if amount % divisor == 0:
            first = divisor
    second = amount // first
    flat_real = real_part.reshape(-1, second, first)
    flat_imag = imag_part.reshape(-1, second, first)
    cos_second, sin_second = phase_tables(second, second, second, sign)
    section_real, section_imag = complex_apply(
        flat_real, flat_imag, cos_second, sin_second, "pmn,mk->pkn"
    )
    twist_cos, twist_sin = phase_tables(second, first, amount, sign)
    turned_real = section_real * twist_cos - section_imag * twist_sin
    turned_imag = section_real * twist_sin + section_imag * twist_cos
    cos_first, sin_first = phase_tables(first, first, first, sign)
    final_real, final_imag = complex_apply(
        turned_real, turned_imag, cos_first, sin_first, "pkn,nj->pjk"
    )
    final_real = final_real.reshape(leading + (amount,)) * factor
    final_imag = final_imag.reshape(leading + (amount,)) * factor
    return (final_real, final_imag)


def pick_amplitudes(rows, index, width):
    positions = jnp.arange(width, dtype=jnp.int32)
    onehot = (index[:, :, None] == positions[None, None, :]).astype(jnp.float32)
    return jnp.einsum("pan,ain->pai", rows, onehot, precision=HIGHEST)


def general_body(wave_field, contrast, layer_of_plane, toeplitz_table, hankel_table, layer_rates):
    row_count = wave_field.shape[2]
    width_y = wave_field.shape[3]
    lat_count = lax.axis_size("lat")
    lay_count = lax.axis_size("lay")
    width_x = row_count * lat_count
    ky_band = width_y // lat_count
    table_width = toeplitz_table.shape[-1]
    plane_total = (table_width + 1) // 2
    layer_count = layer_rates.shape[0]
    spec_real, spec_imag = fourier_last(wave_field[0], wave_field[1], -1.0, 1.0)
    along_y = jnp.stack([spec_real, spec_imag], 2)
    freq_x = signed_of(jnp.arange(width_x, dtype=jnp.int32), width_x)
    ky_first = lax.axis_index("lat") * ky_band
    layer_ids = jnp.arange(layer_count, dtype=jnp.int32)

    def couple(z_out, z_in, source, ky_rows):
        onehot = (layer_of_plane[z_out][:, None] == layer_ids[None, :]).astype(jnp.float32)
        rate_out = jnp.dot(onehot, layer_rates, precision=HIGHEST)
        rows_toeplitz = jnp.einsum("al,pln->pan", onehot, toeplitz_table, precision=HIGHEST)
        rows_hankel = jnp.einsum("al,pln->pan", onehot, hankel_table, precision=HIGHEST)
        offset = z_out[:, None] - z_in[None, :]
        plane_sum = z_out[:, None] + z_in[None, :]
        amp_toeplitz = pick_amplitudes(rows_toeplitz, offset + plane_total - 1, table_width)
        amp_hankel = pick_amplitudes(rows_hankel, plane_sum, table_width)
        freq_y = signed_of(ky_rows, width_y)
        steepness = jnp.sqrt(1.0 + freq_y[:, None] ** 2 + freq_x[None, :] ** 2)
        scaled = rate_out[:, None, None, None] * steepness[None, None] / plane_total
        decay_toeplitz = jnp.exp(-scaled * jnp.abs(offset).astype(jnp.float32)[:, :, None, None])
        decay_hankel = jnp.exp(-scaled * (0.5 * plane_sum.astype(jnp.float32))[:, :, None, None])
        kern_real = (
            amp_toeplitz[0][:, :, None, None] * decay_toeplitz
            + amp_hankel[0][:, :, None, None] * decay_hankel
        )
        kern_imag = (
            amp_toeplitz[1][:, :, None, None] * decay_toeplitz
            + amp_hankel[1][:, :, None, None] * decay_hankel
        )
        real_src = source[None, :, 0]
        imag_src = source[None, :, 1]
        out_real = jnp.sum(kern_real * real_src - kern_imag * imag_src, axis=1)
        out_imag = jnp.sum(kern_real * imag_src + kern_imag * real_src, axis=1)
        return jnp.stack([out_real, out_imag], 1)

    narrow = ky_band // lay_count
    narrow_rows = ky_first + lax.axis_index("lay") * narrow + jnp.arange(narrow, dtype=jnp.int32)
    lines_in = lax.all_to_all(along_y, "lat", split_axis=3, concat_axis=1, tiled=True)
    line_real = jnp.transpose(lines_in[:, :, 0], (0, 2, 1))
    line_imag = jnp.transpose(lines_in[:, :, 1], (0, 2, 1))
    out_real, out_imag = fourier_last(line_real, line_imag, -1.0, 1.0)
    spectrum = jnp.stack([out_real, out_imag], 1)
    gathered = lax.all_to_all(spectrum, "lay", split_axis=2, concat_axis=0, tiled=True)
    all_planes = gathered.shape[0]
    every_plane = jnp.arange(all_planes, dtype=jnp.int32)
    block_size = math.gcd(all_planes, 8)

    def one_block(which):
        z_out = which * block_size + jnp.arange(block_size, dtype=jnp.int32)
        return couple(z_out, every_plane, gathered, narrow_rows)

    stacked = lax.map(one_block, jnp.arange(all_planes // block_size, dtype=jnp.int32))
    coupled = stacked.reshape(all_planes, 2, narrow_rows.shape[0], width_x)
    mixed = lax.all_to_all(coupled, "lay", split_axis=0, concat_axis=2, tiled=True)
    out_real, out_imag = fourier_last(mixed[:, 0], mixed[:, 1], 1.0, 1.0 / width_x)
    spatial_x = jnp.transpose(jnp.stack([out_real, out_imag], 1), (0, 3, 1, 2))
    lines = lax.all_to_all(spatial_x, "lat", split_axis=1, concat_axis=3, tiled=True)
    space_real, space_imag = fourier_last(lines[:, :, 0], lines[:, :, 1], 1.0, 1.0 / width_y)
    return jnp.stack([space_real, space_imag], 0) * contrast[None]


LANES = 128
SUBLANES = 8
MESH = pl.DeviceIdType.MESH


def split_tables(amount):
    half = amount // 2
    index = np.arange(half)
    angle = 2.0 * np.pi / half * (index[:, None] * index[None, :] % half)
    cos_part, sin_part = np.cos(angle), np.sin(angle)
    right = np.block([[cos_part, -sin_part], [sin_part, cos_part]]).astype(np.float32)
    high = right.astype(jnp.bfloat16)
    low = (right - high.astype(np.float32)).astype(jnp.bfloat16)
    turn = 2.0 * np.pi / amount * index
    twiddle = np.stack([np.cos(turn), np.sin(turn)]).astype(np.float32)
    return high, low, np.ascontiguousarray(high.T), np.ascontiguousarray(low.T), twiddle


def split(value):
    high = value.astype(jnp.bfloat16)
    return high, (value - high.astype(jnp.float32)).astype(jnp.bfloat16)


def product(left, right, contract):
    dot = functools.partial(
        lax.dot_general,
        dimension_numbers=(contract, ((), ())),
        preferred_element_type=jnp.float32,
    )
    return dot(left[0], right[0]) + (dot(left[1], right[0]) + dot(left[0], right[1]))


def swap_halves(first, second):
    low = lax.broadcasted_iota(jnp.int32, first.shape, first.ndim - 1) < LANES // 2
    one = jnp.where(low, first, pltpu.roll(second, LANES // 2, first.ndim - 1))
    two = jnp.where(low, pltpu.roll(first, LANES // 2, first.ndim - 1), second)
    return one, two


def butterfly_in(real_part, imag_part, twiddle):
    half = real_part.shape[-1] // 2
    cos_row, sin_row = twiddle[0:1, :], twiddle[1:2, :]
    even = (real_part[:, :half] + real_part[:, half:], imag_part[:, :half] + imag_part[:, half:])
    real_gap = real_part[:, :half] - real_part[:, half:]
    imag_gap = imag_part[:, :half] - imag_part[:, half:]
    odd = (
        real_gap * cos_row + imag_gap * sin_row,
        imag_gap * cos_row - real_gap * sin_row,
    )
    return even, odd


def butterfly_out(even, odd, twiddle):
    cos_row, sin_row = twiddle[0:1, :], twiddle[1:2, :]
    real_turn = odd[0] * cos_row - odd[1] * sin_row
    imag_turn = odd[0] * sin_row + odd[1] * cos_row
    real_part = jnp.concatenate([even[0] + real_turn, even[0] - real_turn], 1)
    imag_part = jnp.concatenate([even[1] + imag_turn, even[1] - imag_turn], 1)
    return real_part, imag_part


def couple_kernel(
    lat_count, lay_count, planes, rows,
    layer_ref, rate_ref, toeplitz_ref, hankel_ref,
    field_any, fh_any, fl_any, ih_any, il_any, twiddle_ref,
    out_any,
    send_in, recv_in, send_out, recv_out, field_x, spectrum, mixed, powers, even_y,
    field_ref, fh_ref, fl_ref, ih_ref, il_ref, out_ref,
    send_sem, recv_sem, load_sem, store_sem,
):
    device_count = lat_count * lay_count
    my_lat, my_lay = lax.axis_index("lat"), lax.axis_index("lay")
    me = my_lat * lay_count + my_lay
    lines, width_y = field_ref.shape[1:]
    width_x = rows * lat_count
    half_y, half_x = width_y // 2, width_x // 2
    depth = half_y // device_count
    plane_total = planes * lay_count
    layer_count = rate_ref.shape[0]

    own_step = 0

    def partner(step):
        lat_step = step // lay_count
        to_lat = (my_lat + lat_step) % lat_count
        to_lay = (my_lay + step % lay_count) % lay_count
        return to_lat, to_lay

    def over_all(act):
        def one(step, carry):
            act(step)
            return carry

        lax.fori_loop(0, own_step, one, 0)
        lax.fori_loop(own_step + 1, device_count, one, 0)

    chunk = min(lines, 2 * LANES)
    chunks = lines // chunk
    loads = [
        pltpu.make_async_copy(
            field_any.at[:, pl.ds(i * chunk, chunk)],
            field_ref.at[:, pl.ds(i * chunk, chunk)],
            load_sem.at[i],
        )
        for i in range(chunks)
    ] + [
        pltpu.make_async_copy(source, target, load_sem.at[chunks + i])
        for i, (source, target) in enumerate(
            [(ih_any, ih_ref), (il_any, il_ref), (fh_any, fh_ref), (fl_any, fl_ref)]
        )
    ]
    for i in [0, chunks, chunks + 1, *range(1, chunks), chunks + 2, chunks + 3]:
        loads[i].start()

    barrier = pltpu.get_barrier_semaphore()

    over_all(
        lambda step: pl.semaphore_signal(
            barrier, inc=1, device_id=partner(step), device_id_type=MESH
        )
    )

    def exchange(source, target, part, phase, step):
        to_lat, to_lay = partner(step)
        return pltpu.make_async_remote_copy(
            src_ref=source.at[to_lat * lay_count + to_lay, part],
            dst_ref=target.at[me, part],
            send_sem=send_sem.at[phase, step],
            recv_sem=recv_sem.at[phase, step],
            device_id=(to_lat, to_lay),
            device_id_type=MESH,
        )

    loads[chunks].wait()
    loads[chunks + 1].wait()

    def transform_y(side):
        for start in range(0, lines, chunk):
            where = slice(start, start + chunk)
            if side == 0:
                loads[start // chunk].wait()
            pairs = butterfly_in(field_ref[0, where, :], field_ref[1, where, :], twiddle_ref)
            right = split(jnp.concatenate(pairs[side], 1))
            result = product((ih_ref[...], il_ref[...]), right, ((1,), (1,)))
            for comp in range(2):
                piece = result[comp * half_y:(comp + 1) * half_y]
                send_in[:, side, comp, :, where] = piece.reshape(device_count, depth, chunk)

    for side in range(2):
        transform_y(side)
        if side == 0:
            pl.semaphore_wait(barrier, device_count - 1)
        over_all(lambda step: exchange(send_in, recv_in, side, side, step).start())
        recv_in[me, side] = send_in[me, side]

    def signed(index, amount):
        index = jnp.where(index >= amount // 2, index - amount, index)
        return index.astype(jnp.float32) / (amount / 2)

    tile = (depth, width_x)
    place_x = lax.broadcasted_iota(jnp.int32, tile, 1)
    freq_x = signed(2 * (place_x % half_x) + place_x // half_x, width_x)
    for side in range(2):
        ky = 2 * (me * depth + lax.broadcasted_iota(jnp.int32, tile, 0)) + side
        freq_y = signed(ky, width_y)
        steepness = jnp.sqrt(1.0 + freq_x * freq_x + freq_y * freq_y)

        def one_layer(layer, carry):
            base = jnp.exp(steepness * (-rate_ref[layer] / (2 * plane_total)))

            def one_power(m, value):
                powers[side, layer, m] = value
                return value * base

            lax.fori_loop(0, 2 * plane_total - 1, one_power, jnp.ones(tile, jnp.float32))
            return carry

        lax.fori_loop(0, layer_count, one_layer, 0)

    loads[chunks + 2].wait()
    loads[chunks + 3].wait()

    def load_lines(side):
        def one_lay(lay, carry):
            for pair in range(planes // 2):
                lanes = slice(pair * LANES, (pair + 1) * LANES)
                for block in range(lat_count // 2):
                    first = recv_in[2 * block * lay_count + lay, side, :, :, lanes]
                    second = recv_in[(2 * block + 1) * lay_count + lay, side, :, :, lanes]
                    even, odd = swap_halves(first, second)
                    place = slice(block * LANES, (block + 1) * LANES)
                    field_x[:, lay * planes + 2 * pair, :, place] = even
                    field_x[:, lay * planes + 2 * pair + 1, :, place] = odd
            return carry

        lax.fori_loop(0, lay_count, one_lay, 0)

    group = min(plane_total, LANES // SUBLANES)

    def transform_x(step, carry):
        some = pl.ds(step * group, group)
        flat = (group * depth, width_x)
        pairs = butterfly_in(
            field_x[0, some].reshape(flat), field_x[1, some].reshape(flat), twiddle_ref
        )
        for side, pair in enumerate(pairs):
            left = split(jnp.concatenate(pair, 1))
            result = product(left, (fh_ref[...], fl_ref[...]), ((1,), (0,)))
            for comp in range(2):
                piece = result[:, comp * half_x:(comp + 1) * half_x]
                spectrum[comp, some, :, side * half_x:(side + 1) * half_x] = piece.reshape(
                    group, depth, half_x
                )
        return carry

    lays_step = 2 if lay_count % 2 == 0 else 1
    planes_step = planes * lays_step

    def lay_of(step, within):
        return (my_lay + 1 + step * lays_step + within) % lay_count

    def invert_x():
        sides = []
        for side in range(2):
            place = slice(side * half_x, (side + 1) * half_x)
            flat = (planes_step * depth, half_x)
            left = split(
                jnp.concatenate(
                    [mixed[comp, :, :, place].reshape(flat) for comp in range(2)], 1
                )
            )
            result = product(left, (ih_ref[...], il_ref[...]), ((1,), (0,)))
            sides.append((result[:, :half_x], result[:, half_x:]))
        real_part, imag_part = butterfly_out(sides[0], sides[1], twiddle_ref)
        full = (planes_step, depth, width_x)
        mixed[0] = (real_part * (1.0 / width_x)).reshape(full)
        mixed[1] = (imag_part * (1.0 / width_x)).reshape(full)

    def store_lines(side, lay, within):
        for pair in range(planes // 2):
            lanes = slice(pair * LANES, (pair + 1) * LANES)
            for block in range(lat_count // 2):
                place = slice(block * LANES, (block + 1) * LANES)
                even = mixed[:, within * planes + 2 * pair, :, place]
                odd = mixed[:, within * planes + 2 * pair + 1, :, place]
                first, second = swap_halves(even, odd)
                send_out[2 * block * lay_count + lay, side, :, :, lanes] = first
                send_out[(2 * block + 1) * lay_count + lay, side, :, :, lanes] = second

    def couple(side, lay, within):
        def one_plane(local, carry):
            plane = lay * planes + local
            layer = layer_ref[plane]
            real_sum = jnp.zeros(tile, jnp.float32)
            imag_sum = jnp.zeros(tile, jnp.float32)
            for source in range(plane_total):
                offset = plane - source
                direct = powers[side, layer, 2 * jnp.abs(offset)]
                mirror = powers[side, layer, plane + source]
                at = offset + plane_total - 1
                kern_real = (
                    toeplitz_ref[0, layer, at] * direct
                    + hankel_ref[0, layer, plane + source] * mirror
                )
                kern_imag = (
                    toeplitz_ref[1, layer, at] * direct
                    + hankel_ref[1, layer, plane + source] * mirror
                )
                real_src, imag_src = spectrum[0, source], spectrum[1, source]
                real_sum += kern_real * real_src - kern_imag * imag_src
                imag_sum += kern_real * imag_src + kern_imag * real_src
            mixed[0, within * planes + local] = real_sum
            mixed[1, within * planes + local] = imag_sum
            return carry

        lax.fori_loop(0, planes, one_plane, 0)

    for side in range(2):
        phase = 2 + side
        over_all(lambda step: exchange(send_in, recv_in, side, side, step).wait_recv())
        load_lines(side)
        lax.fori_loop(0, plane_total // group, transform_x, 0)

        def one_step(step, carry):
            for within in range(lays_step):
                couple(side, lay_of(step, within), within)
            invert_x()
            for within in range(lays_step):
                store_lines(side, lay_of(step, within), within)
            for within in range(lays_step):
                turn = (1 + step * lays_step + within) % lay_count

                def one_lat(lat_step, carry):
                    to = lat_step * lay_count + turn

                    @pl.when(to != own_step)
                    def _():
                        exchange(send_out, recv_out, side, phase, to).start()

                    return carry

                lax.fori_loop(0, lat_count, one_lat, 0)
            return carry

        lax.fori_loop(0, lay_count // lays_step, one_step, 0)
        recv_out[me, side] = send_out[me, side]

    def invert_y(side, where):
        stack = jnp.concatenate(
            [recv_out[:, side, comp, :, where].reshape(half_y, LANES) for comp in range(2)], 0
        )
        result = product((fh_ref[...], fl_ref[...]), split(stack), ((1,), (0,)))
        return result[:half_y].T, result[half_y:].T

    over_all(lambda step: exchange(send_out, recv_out, 0, 2, step).wait_recv())
    for start in range(0, lines, LANES):
        where = slice(start, start + LANES)
        even_y[0, where], even_y[1, where] = invert_y(0, where)
    for side in range(2):
        over_all(lambda step: exchange(send_in, recv_in, side, side, step).wait_send())
    over_all(lambda step: exchange(send_out, recv_out, 0, 2, step).wait_send())
    over_all(lambda step: exchange(send_out, recv_out, 1, 3, step).wait_recv())
    stores = []
    for start in range(0, lines, LANES):
        where = pl.ds(start, LANES)
        odd = invert_y(1, where)
        real_part, imag_part = butterfly_out((even_y[0, where], even_y[1, where]), odd, twiddle_ref)
        out_ref[0, where] = real_part * (1.0 / width_y)
        out_ref[1, where] = imag_part * (1.0 / width_y)
        stores.append(
            pltpu.make_async_copy(
                out_ref.at[:, where], out_any.at[:, where], store_sem.at[start // LANES]
            )
        )
        stores[-1].start()
    for store in stores:
        store.wait()
    over_all(lambda step: exchange(send_out, recv_out, 1, 3, step).wait_send())


def fast_body(wave_field, contrast, layer_of_plane, toeplitz_table, hankel_table, layer_rates):
    _, planes, rows, width_y = wave_field.shape
    lat_count, lay_count = lax.axis_size("lat"), lax.axis_size("lay")
    device_count = lat_count * lay_count
    width_x = rows * lat_count
    depth = width_y // (2 * device_count)
    plane_total = planes * lay_count
    layer_count = layer_rates.shape[0]
    lines = planes * rows
    fh, fl, ih, il, twiddle = (jnp.asarray(t) for t in split_tables(width_y))
    smem = pl.BlockSpec(memory_space=pltpu.SMEM)
    vmem = pl.BlockSpec(memory_space=pltpu.VMEM)
    anywhere = pl.BlockSpec(memory_space=pl.ANY)
    exchanged = (device_count, 2, 2, depth, lines)
    tile_all = (2, plane_total, depth, width_x)
    lays_step = 2 if lay_count % 2 == 0 else 1
    space = pl.pallas_call(
        functools.partial(couple_kernel, lat_count, lay_count, planes, rows),
        out_shape=jax.ShapeDtypeStruct((2, lines, width_y), jnp.float32),
        in_specs=[smem] * 4 + [anywhere] * 5 + [vmem],
        out_specs=anywhere,
        scratch_shapes=[
            pltpu.VMEM(exchanged, jnp.float32),
            pltpu.VMEM(exchanged, jnp.float32),
            pltpu.VMEM(exchanged, jnp.float32),
            pltpu.VMEM(exchanged, jnp.float32),
            pltpu.VMEM(tile_all, jnp.float32),
            pltpu.VMEM(tile_all, jnp.float32),
            pltpu.VMEM((2, planes * lays_step, depth, width_x), jnp.float32),
            pltpu.VMEM((2, layer_count, 2 * plane_total - 1, depth, width_x), jnp.float32),
            pltpu.VMEM((2, lines, width_y // 2), jnp.float32),
            pltpu.VMEM((2, lines, width_y), jnp.float32),
            pltpu.VMEM(fh.shape, fh.dtype),
            pltpu.VMEM(fl.shape, fl.dtype),
            pltpu.VMEM(ih.shape, ih.dtype),
            pltpu.VMEM(il.shape, il.dtype),
            pltpu.VMEM((2, lines, width_y), jnp.float32),
            pltpu.SemaphoreType.DMA((4, device_count)),
            pltpu.SemaphoreType.DMA((4, device_count)),
            pltpu.SemaphoreType.DMA((lines // min(lines, 2 * LANES) + 4,)),
            pltpu.SemaphoreType.DMA((lines // LANES,)),
        ],
        compiler_params=pltpu.CompilerParams(
            collective_id=0, has_side_effects=True, vmem_limit_bytes=60 * 1024 * 1024
        ),
        name="couple",
    )(
        layer_of_plane, layer_rates, toeplitz_table, hankel_table,
        wave_field.reshape(2, lines, width_y), fh, fl, ih, il, twiddle,
    )
    return space.reshape(wave_field.shape) * contrast[None]


def body(wave_field, *others):
    _, planes, rows, width_y = wave_field.shape
    lat_count, lay_count = lax.axis_size("lat"), lax.axis_size("lay")
    device_count = lat_count * lay_count
    width_x = rows * lat_count
    fits = (
        2 * rows == LANES
        and planes % 2 == 0
        and width_x == width_y
        and width_y % (4 * LANES) == 0
        and width_y == 2 * device_count * SUBLANES
        and device_count % 2 == 0
        and lat_count % 2 == 0
        and (planes * lay_count) % (LANES // SUBLANES) == 0
        and (planes * rows) % (2 * LANES) == 0
    )
    return (fast_body if fits else general_body)(wave_field, *others)


def solution(mesh):
    return jax.shard_map(
        body,
        mesh=mesh,
        in_specs=(P(None, "lay", "lat", None), P("lay", "lat", None), P(), P(), P(), P()),
        out_specs=P(None, "lay", "lat", None),
        check_vma=False,
    )
```

profile of v0, /device:TPU:0, one launch (start us, length us, event | category | flops | bytes accessed | tf_op | source)
XLA Modules:
  0.0 108.3 jit_solution(2075623034221818109)
XLA Ops:
  0.0 0.0 copy-start
  0.0 104.9 %couple.1 = f32[2,512,512]{2,1,0:T(8,128)} custom-call(s32[32]{0:T(128)} %layer_ref.1, f32[8]{0:T(128)} %rate_ref.1, f32[2,8,63]{2,1,0:T(8,128)} %toeplitz_ref.1, f32[2,8,63]{2,1,0:T(8,128)} %hankel_ref.1, f32[2,512,512]{2,1,0:T(8,128)} %bitcast.3, bf16[512,512]{1,0:T(8,128)(2,1)} %constant.10.clone.fh_any, bf16[512,512]{1,0:T(8,128)(2,1)} %constant.11.clone.fl_any, ...), custom_call_target="tpu_custom_call" | custom-call | tf_op jit(solution)/shard_map/couple/pallas_call | solution.py:495
  104.9 0.0 copy-done
  104.9 3.3 %broadcast_multiply_fusion = f32[2,8,64,512]{3,2,1,0:T(8,128)} fusion(f32[2,8,64,512]{3,2,1,0:T(8,128)} %bitcast.2, f32[8,64,512]{2,1,0:T(8,128)S(1)} %copy-done), kind=kLoop, calls=%fused_computation | loop fusion | flops 524288 | bytes 5242880 | tf_op jit(solution)/shard_map/mul | solution.py:529
Async XLA Ops:
  0.0 104.9 %copy-start = (f32[8,64,512]{2,1,0:T(8,128)S(1)}, f32[8,64,512]{2,1,0:T(8,128)}, u32[]{:S(2)}) copy-start(f32[8,64,512]{2,1,0:T(8,128)} %param.12) | copy-start | bytes 3145732
where the time goes:
time: 108 us
  Pallas kernels  105 us (97%)
  other arithmetic  3.33 us (3%)
    pallas_call x1, Pallas kernels, fast_body(): pl.pallas_call(functools.partial(couple_kernel, lat_count, lay_count, pla...  105 us
    mul x1, other arithmetic, fast_body(): return space.reshape(wave_field.shape) * contrast[None]  3.33 us

commit v1 on v0

--- a/solution.py
+++ b/solution.py
@@ -141,17 +141,35 @@
 MESH = pl.DeviceIdType.MESH
 
 
+def split_pair(table):
+    table = table.astype(np.float32)
+    high = table.astype(jnp.bfloat16)
+    return high, (table - high.astype(np.float32)).astype(jnp.bfloat16)
+
+
 def split_tables(amount):
     half = amount // 2
     index = np.arange(half)
     angle = 2.0 * np.pi / half * (index[:, None] * index[None, :] % half)
     cos_part, sin_part = np.cos(angle), np.sin(angle)
-    right = np.block([[cos_part, -sin_part], [sin_part, cos_part]]).astype(np.float32)
-    high = right.astype(jnp.bfloat16)
-    low = (right - high.astype(np.float32)).astype(jnp.bfloat16)
+    right = np.block([[cos_part, -sin_part], [sin_part, cos_part]])
+    high, low = split_pair(right)
     turn = 2.0 * np.pi / amount * index
     twiddle = np.stack([np.cos(turn), np.sin(turn)]).astype(np.float32)
     return high, low, np.ascontiguousarray(high.T), np.ascontiguousarray(low.T), twiddle
+
+
+def class_tables(amount, classes):
+    length = amount // classes
+    index = np.arange(length)
+    every = []
+    for which in range(classes):
+        turns = (which + classes * index[:, None]) * index[None, :] % amount
+        angle = 2.0 * np.pi / amount * turns
+        cos_part, sin_part = np.cos(angle), np.sin(angle)
+        forward = np.block([[cos_part, sin_part], [-sin_part, cos_part]])
+        every.append(np.stack([*split_pair(forward), *split_pair(forward.T)]))
+    return np.stack(every).reshape(2, classes // 2, 4, 2 * length, 2 * length)
 
 
 def split(value):
@@ -197,42 +215,111 @@
     return real_part, imag_part
 
 
+ROOT_HALF = math.sqrt(0.5)
+
+
+def turn_eighths(pair, which, sign):
+    if which == 0:
+        return pair
+    low = lax.broadcasted_iota(jnp.int32, pair.shape, pair.ndim - 1) < LANES // 2
+    other = pltpu.roll(pair, LANES // 2, pair.ndim - 1)
+    crossed = jnp.where(low, other, -other) if sign < 0 else jnp.where(low, -other, other)
+    if which == 2:
+        return crossed
+    return ROOT_HALF * (crossed + pair) if which == 1 else ROOT_HALF * (crossed - pair)
+
+
+def fold_classes(real_parts, imag_parts):
+    def plus(first, second):
+        return tuple(parts[first] + parts[second] for parts in (real_parts, imag_parts))
+
+    def minus(first, second):
+        return tuple(parts[first] - parts[second] for parts in (real_parts, imag_parts))
+
+    sum_even, sum_odd, gap_even, gap_odd = plus(0, 2), plus(1, 3), minus(0, 2), minus(1, 3)
+    fours = [
+        (sum_even[0] + sum_odd[0], sum_even[1] + sum_odd[1]),
+        (gap_even[0] + gap_odd[1], gap_even[1] - gap_odd[0]),
+        (sum_even[0] - sum_odd[0], sum_even[1] - sum_odd[1]),
+        (gap_even[0] - gap_odd[1], gap_even[1] + gap_odd[0]),
+    ]
+    sides = []
+    for which, (real_part, imag_part) in enumerate(fours):
+        near, far = swap_halves(real_part, imag_part)
+        far = turn_eighths(far, which, -1)
+        sides.append((near + far, near - far))
+    return sides
+
+
+def unfold_classes(sides):
+    fours = []
+    for which, (first, second) in enumerate(sides):
+        near, far = first + second, turn_eighths(first - second, which, 1)
+        fours.append(swap_halves(near, far))
+    sum_even = [fours[0][i] + fours[2][i] for i in range(2)]
+    gap_even = [fours[0][i] - fours[2][i] for i in range(2)]
+    sum_odd = [fours[1][i] + fours[3][i] for i in range(2)]
+    gap_odd = [fours[1][i] - fours[3][i] for i in range(2)]
+    return [
+        (sum_even[0] + sum_odd[0], sum_even[1] + sum_odd[1]),
+        (gap_even[0] - gap_odd[1], gap_even[1] + gap_odd[0]),
+        (sum_even[0] - sum_odd[0], sum_even[1] - sum_odd[1]),
+        (gap_even[0] + gap_odd[1], gap_even[1] - gap_odd[0]),
+    ]
+
+
+ORDER = (3, 2, 1)
+
+
 def couple_kernel(
     lat_count, lay_count, planes, rows,
     layer_ref, rate_ref, toeplitz_ref, hankel_ref,
-    field_any, fh_any, fl_any, ih_any, il_any, twiddle_ref,
-    out_any,
-    send_in, recv_in, send_out, recv_out, field_x, spectrum, mixed, powers, even_y,
-    field_ref, fh_ref, fl_ref, ih_ref, il_ref, out_ref,
-    send_sem, recv_sem, load_sem, store_sem,
+    field_any, fh_any, fl_any, ih_any, il_any, tables_any, twiddle_ref,
+    out_ref,
+    send_fold, recv_fold, send_in, recv_in, send_out, recv_mid, send_fin, recv_fin,
+    field_x, spectrum, mixed, powers,
+    field_ref, fh_ref, fl_ref, ih_ref, il_ref, tables_ref,
+    fold_send, fold_recv, in_send, in_recv, out_send, out_recv, fin_send, fin_recv, load_sem,
 ):
-    device_count = lat_count * lay_count
+    inner = 2
+    outer = lat_count // inner
+    peers = inner * lay_count
     my_lat, my_lay = lax.axis_index("lat"), lax.axis_index("lay")
-    me = my_lat * lay_count + my_lay
+    my_outer = my_lat // inner
+    my_peer = my_lat % inner * lay_count + my_lay
     lines, width_y = field_ref.shape[1:]
     width_x = rows * lat_count
-    half_y, half_x = width_y // 2, width_x // 2
-    depth = half_y // device_count
+    half_x = width_x // 2
+    classes = 2 * outer
+    length = width_y // classes
+    depth = length // peers
     plane_total = planes * lay_count
     layer_count = rate_ref.shape[0]
-
-    own_step = 0
-
-    def partner(step):
-        lat_step = step // lay_count
-        to_lat = (my_lat + lat_step) % lat_count
-        to_lay = (my_lay + step % lay_count) % lay_count
-        return to_lat, to_lay
-
-    def over_all(act):
+    pairs = planes // 2
+
+    def column(way):
+        low = (my_outer % 2 + way % 2) % 2
+        high = (my_outer // 2 + way // 2) % 2
+        return 2 * high + low
+
+    def column_id(way):
+        return column(way) * inner + my_lat % inner, my_lay
+
+    def peer(step):
+        return (my_peer + step) % peers
+
+    def peer_id(step):
+        to = peer(step)
+        return my_outer * inner + to // lay_count, to % lay_count
+
+    def over_peers(act):
         def one(step, carry):
             act(step)
             return carry
 
-        lax.fori_loop(0, own_step, one, 0)
-        lax.fori_loop(own_step + 1, device_count, one, 0)
-
-    chunk = min(lines, 2 * LANES)
+        lax.fori_loop(1, peers, one, 0)
+
+    chunk = LANES
     chunks = lines // chunk
     loads = [
         pltpu.make_async_copy(
@@ -244,52 +331,91 @@
     ] + [
         pltpu.make_async_copy(source, target, load_sem.at[chunks + i])
         for i, (source, target) in enumerate(
-            [(ih_any, ih_ref), (il_any, il_ref), (fh_any, fh_ref), (fl_any, fl_ref)]
+            [
+                (tables_any.at[0, my_outer], tables_ref.at[0]),
+                (tables_any.at[1, my_outer], tables_ref.at[1]),
+                (fh_any, fh_ref), (fl_any, fl_ref), (ih_any, ih_ref), (il_any, il_ref),
+            ]
         )
     ]
-    for i in [0, chunks, chunks + 1, *range(1, chunks), chunks + 2, chunks + 3]:
-        loads[i].start()
+    for load in loads:
+        load.start()
 
     barrier = pltpu.get_barrier_semaphore()
-
-    over_all(
+    for way in range(1, outer):
+        pl.semaphore_signal(barrier, inc=1, device_id=column_id(way), device_id_type=MESH)
+    over_peers(
         lambda step: pl.semaphore_signal(
-            barrier, inc=1, device_id=partner(step), device_id_type=MESH
-        )
-    )
-
-    def exchange(source, target, part, phase, step):
-        to_lat, to_lay = partner(step)
+            barrier, inc=1, device_id=peer_id(step), device_id_type=MESH
+        )
+    )
+
+    def remote(source, target, sems, index, device):
         return pltpu.make_async_remote_copy(
-            src_ref=source.at[to_lat * lay_count + to_lay, part],
-            dst_ref=target.at[me, part],
-            send_sem=send_sem.at[phase, step],
-            recv_sem=recv_sem.at[phase, step],
-            device_id=(to_lat, to_lay),
+            src_ref=source,
+            dst_ref=target,
+            send_sem=sems[0].at[index],
+            recv_sem=sems[1].at[index],
+            device_id=device,
             device_id_type=MESH,
         )
+
+    def fold_copy(side, way):
+        return remote(
+            send_fold.at[column(way), side], recv_fold.at[my_outer, side],
+            (fold_send, fold_recv), (side, way), column_id(way),
+        )
+
+    def in_copy(origin, side, step):
+        return remote(
+            send_in.at[peer(step), origin, side], recv_in.at[origin, my_peer, side],
+            (in_send, in_recv), (origin, side, step), peer_id(step),
+        )
+
+    def out_copy(side, pair, step):
+        return remote(
+            send_out.at[peer(step), side, pair], recv_mid.at[my_peer, side, pair],
+            (out_send, out_recv), (side, pair, step), peer_id(step),
+        )
+
+    def fin_copy(side, pair, way):
+        return remote(
+            send_fin.at[column(way), side, pair], recv_fin.at[my_outer, side, pair],
+            (fin_send, fin_recv), (side, pair, way), column_id(way),
+        )
+
+    for i in range(chunks):
+        where = slice(i * chunk, (i + 1) * chunk)
+        loads[i].wait()
+        parts = [
+            [field_ref[comp, where, t * LANES:(t + 1) * LANES] for t in range(outer)]
+            for comp in range(2)
+        ]
+        for which, both in enumerate(fold_classes(*parts)):
+            for side in range(2):
+                send_fold[which, side, where] = both[side]
+
+    pl.semaphore_wait(barrier, outer - 1 + peers - 1)
+    for side in range(2):
+        for way in ORDER:
+            fold_copy(side, way).start()
 
     loads[chunks].wait()
     loads[chunks + 1].wait()
 
-    def transform_y(side):
-        for start in range(0, lines, chunk):
-            where = slice(start, start + chunk)
-            if side == 0:
-                loads[start // chunk].wait()
-            pairs = butterfly_in(field_ref[0, where, :], field_ref[1, where, :], twiddle_ref)
-            right = split(jnp.concatenate(pairs[side], 1))
-            result = product((ih_ref[...], il_ref[...]), right, ((1,), (1,)))
+    def transform_y(source, origin, side):
+        for start in range(0, lines, 2 * LANES):
+            where = slice(start, start + 2 * LANES)
+            right = split(source[origin, side, where])
+            result = product((tables_ref[side, 0], tables_ref[side, 1]), right, ((1,), (1,)))
             for comp in range(2):
-                piece = result[comp * half_y:(comp + 1) * half_y]
-                send_in[:, side, comp, :, where] = piece.reshape(device_count, depth, chunk)
+                piece = result[comp * length:(comp + 1) * length]
+                send_in[:, origin, side, comp, :, where] = piece.reshape(peers, depth, 2 * LANES)
+        over_peers(lambda step: in_copy(origin, side, step).start())
+        recv_in[origin, my_peer, side] = send_in[my_peer, origin, side]
 
     for side in range(2):
-        transform_y(side)
-        if side == 0:
-            pl.semaphore_wait(barrier, device_count - 1)
-        over_all(lambda step: exchange(send_in, recv_in, side, side, step).start())
-        recv_in[me, side] = send_in[me, side]
+        transform_y(send_fold, my_outer, side)
 
     def signed(index, amount):
         index = jnp.where(index >= amount // 2, index - amount, index)
@@ -299,8 +425,8 @@
     place_x = lax.broadcasted_iota(jnp.int32, tile, 1)
     freq_x = signed(2 * (place_x % half_x) + place_x // half_x, width_x)
     for side in range(2):
-        ky = 2 * (me * depth + lax.broadcasted_iota(jnp.int32, tile, 0)) + side
-        freq_y = signed(ky, width_y)
+        place_y = my_peer * depth + lax.broadcasted_iota(jnp.int32, tile, 0)
+        freq_y = signed(classes * place_y + my_outer + outer * side, width_y)
         steepness = jnp.sqrt(1.0 + freq_x * freq_x + freq_y * freq_y)
 
         def one_layer(layer, carry):
@@ -315,16 +441,23 @@
 
         lax.fori_loop(0, layer_count, one_layer, 0)
 
-    loads[chunks + 2].wait()
-    loads[chunks + 3].wait()
+    for i in range(chunks + 2, chunks + 6):
+        loads[i].wait()
+
+    def gather(side, way):
+        fold_copy(side, way).wait_recv()
+        transform_y(recv_fold, column(way), side)
+
+    for way in ORDER:
+        gather(0, way)
 
     def load_lines(side):
         def one_lay(lay, carry):
-            for pair in range(planes // 2):
+            for pair in range(pairs):
                 lanes = slice(pair * LANES, (pair + 1) * LANES)
-                for block in range(lat_count // 2):
-                    first = recv_in[2 * block * lay_count + lay, side, :, :, lanes]
-                    second = recv_in[(2 * block + 1) * lay_count + lay, side, :, :, lanes]
+                for block in range(outer):
+                    first = recv_in[block, lay, side, :, :, lanes]
+                    second = recv_in[block, lay_count + lay, side, :, :, lanes]
                     even, odd = swap_halves(first, second)
                     place = slice(block * LANES, (block + 1) * LANES)
                     field_x[:, lay * planes + 2 * pair, :, place] = even
@@ -338,56 +471,51 @@
     def transform_x(step, carry):
         some = pl.ds(step * group, group)
         flat = (group * depth, width_x)
-        pairs = butterfly_in(
+        halves = butterfly_in(
             field_x[0, some].reshape(flat), field_x[1, some].reshape(flat), twiddle_ref
         )
-        for side, pair in enumerate(pairs):
+        for half, pair in enumerate(halves):
             left = split(jnp.concatenate(pair, 1))
             result = product(left, (fh_ref[...], fl_ref[...]), ((1,), (0,)))
             for comp in range(2):
                 piece = result[:, comp * half_x:(comp + 1) * half_x]
-                spectrum[comp, some, :, side * half_x:(side + 1) * half_x] = piece.reshape(
+                spectrum[comp, some, :, half * half_x:(half + 1) * half_x] = piece.reshape(
                     group, depth, half_x
                 )
         return carry
 
-    lays_step = 2 if lay_count % 2 == 0 else 1
-    planes_step = planes * lays_step
-
-    def lay_of(step, within):
-        return (my_lay + 1 + step * lays_step + within) % lay_count
+    some_planes = 2 * lay_count
 
     def invert_x():
-        sides = []
-        for side in range(2):
-            place = slice(side * half_x, (side + 1) * half_x)
-            flat = (planes_step * depth, half_x)
+        halves = []
+        for half in range(2):
+            place = slice(half * half_x, (half + 1) * half_x)
+            flat = (some_planes * depth, half_x)
             left = split(
                 jnp.concatenate(
                     [mixed[comp, :, :, place].reshape(flat) for comp in range(2)], 1
                 )
             )
             result = product(left, (ih_ref[...], il_ref[...]), ((1,), (0,)))
-            sides.append((result[:, :half_x], result[:, half_x:]))
-        real_part, imag_part = butterfly_out(sides[0], sides[1], twiddle_ref)
-        full = (planes_step, depth, width_x)
-        mixed[0] = (real_part * (1.0 / width_x)).reshape(full)
-        mixed[1] = (imag_part * (1.0 / width_x)).reshape(full)
-
-    def store_lines(side, lay, within):
-        for pair in range(planes // 2):
-            lanes = slice(pair * LANES, (pair + 1) * LANES)
-            for block in range(lat_count // 2):
+            halves.append((result[:, :half_x], result[:, half_x:]))
+        real_part, imag_part = butterfly_out(halves[0], halves[1], twiddle_ref)
+        full = (some_planes, depth, width_x)
+        factor = 1.0 / (width_x * width_y)
+        mixed[0] = (real_part * factor).reshape(full)
+        mixed[1] = (imag_part * factor).reshape(full)
+
+    def store_lines(side, pair):
+        for lay in range(lay_count):
+            for block in range(outer):
                 place = slice(block * LANES, (block + 1) * LANES)
-                even = mixed[:, within * planes + 2 * pair, :, place]
-                odd = mixed[:, within * planes + 2 * pair + 1, :, place]
+                even, odd = mixed[:, 2 * lay, :, place], mixed[:, 2 * lay + 1, :, place]
                 first, second = swap_halves(even, odd)
-                send_out[2 * block * lay_count + lay, side, :, :, lanes] = first
-                send_out[(2 * block + 1) * lay_count + lay, side, :, :, lanes] = second
-
-    def couple(side, lay, within):
-        def one_plane(local, carry):
-            plane = lay * planes + local
+                send_out[lay, side, pair, :, :, place] = first
+                send_out[lay_count + lay, side, pair, :, :, place] = second
+
+    def couple(side, pair):
+        def one_plane(place, carry):
+            plane = place // 2 * planes + 2 * pair + place % 2
             layer = layer_ref[plane]
             real_sum = jnp.zeros(tile, jnp.float32)
             imag_sum = jnp.zeros(tile, jnp.float32)
@@ -407,124 +535,148 @@
                 real_src, imag_src = spectrum[0, source], spectrum[1, source]
                 real_sum += kern_real * real_src - kern_imag * imag_src
                 imag_sum += kern_real * imag_src + kern_imag * real_src
-            mixed[0, within * planes + local] = real_sum
-            mixed[1, within * planes + local] = imag_sum
+            mixed[0, place] = real_sum
+            mixed[1, place] = imag_sum
             return carry
 
-        lax.fori_loop(0, planes, one_plane, 0)
+        lax.fori_loop(0, some_planes, one_plane, 0)
+
+    def invert_y(side, pair):
+        over_peers(lambda step: out_copy(side, pair, step).wait_recv())
+        stack = jnp.concatenate(
+            [recv_mid[:, side, pair, comp].reshape(length, outer * LANES) for comp in range(2)], 0
+        )
+        result = product((tables_ref[side, 2], tables_ref[side, 3]), split(stack), ((1,), (0,)))
+        for block in range(outer):
+            send_fin[block, side, pair] = result[:, block * LANES:(block + 1) * LANES].T
+        for way in ORDER:
+            fin_copy(side, pair, way).start()
+        recv_fin[my_outer, side, pair] = send_fin[my_outer, side, pair]
 
     for side in range(2):
-        phase = 2 + side
-        over_all(lambda step: exchange(send_in, recv_in, side, side, step).wait_recv())
+        for origin in range(outer):
+            over_peers(lambda step: in_copy(origin, side, step).wait_recv())
         load_lines(side)
         lax.fori_loop(0, plane_total // group, transform_x, 0)
 
-        def one_step(step, carry):
-            for within in range(lays_step):
-                couple(side, lay_of(step, within), within)
+        def one_pair(pair, carry):
+            couple(side, pair)
             invert_x()
-            for within in range(lays_step):
-                store_lines(side, lay_of(step, within), within)
-            for within in range(lays_step):
-                turn = (1 + step * lays_step + within) % lay_count
-
-                def one_lat(lat_step, carry):
-                    to = lat_step * lay_count + turn
-
-                    @pl.when(to != own_step)
-                    def _():
-                        exchange(send_out, recv_out, side, phase, to).start()
-
-                    return carry
-
-                lax.fori_loop(0, lat_count, one_lat, 0)
+            store_lines(side, pair)
+            over_peers(lambda step: out_copy(side, pair, step).start())
+            recv_mid[my_peer, side, pair] = send_out[my_peer, side, pair]
+
+            @pl.when(pair >= 1)
+            def _():
+                invert_y(side, pair - 1)
+
+            if side == 0:
+
+                @pl.when(pair == pairs - 2)
+                def _():
+                    gather(1, ORDER[0])
+
+                @pl.when(pair == pairs - 1)
+                def _():
+                    gather(1, ORDER[1])
+
             return carry
 
-        lax.fori_loop(0, lay_count // lays_step, one_step, 0)
-        recv_out[me, side] = send_out[me, side]
-
-    def invert_y(side, where):
-        stack = jnp.concatenate(
-            [recv_out[:, side, comp, :, where].reshape(half_y, LANES) for comp in range(2)], 0
-        )
-        result = product((fh_ref[...], fl_ref[...]), split(stack), ((1,), (0,)))
-        return result[:half_y].T, result[half_y:].T
-
-    over_all(lambda step: exchange(send_out, recv_out, 0, 2, step).wait_recv())
-    for start in range(0, lines, LANES):
-        where = slice(start, start + LANES)
-        even_y[0, where], even_y[1, where] = invert_y(0, where)
+        lax.fori_loop(0, pairs, one_pair, 0)
+        invert_y(side, pairs - 1)
+        if side == 0:
+            gather(1, ORDER[2])
+
     for side in range(2):
-        over_all(lambda step: exchange(send_in, recv_in, side, side, step).wait_send())
-    over_all(lambda step: exchange(send_out, recv_out, 0, 2, step).wait_send())
-    over_all(lambda step: exchange(send_out, recv_out, 1, 3, step).wait_recv())
-    stores = []
-    for start in range(0, lines, LANES):
-        where = pl.ds(start, LANES)
-        odd = invert_y(1, where)
-        real_part, imag_part = butterfly_out((even_y[0, where], even_y[1, where]), odd, twiddle_ref)
-        out_ref[0, where] = real_part * (1.0 / width_y)
-        out_ref[1, where] = imag_part * (1.0 / width_y)
-        stores.append(
-            pltpu.make_async_copy(
-                out_ref.at[:, where], out_any.at[:, where], store_sem.at[start // LANES]
-            )
-        )
-        stores[-1].start()
-    for store in stores:
-        store.wait()
-    over_all(lambda step: exchange(send_out, recv_out, 1, 3, step).wait_send())
+        for way in ORDER:
+            fold_copy(side, way).wait_send()
+        for origin in range(outer):
+            over_peers(lambda step: in_copy(origin, side, step).wait_send())
+
+        def sent(pair, carry):
+            over_peers(lambda step: out_copy(side, pair, step).wait_send())
+            return carry
+
+        lax.fori_loop(0, pairs, sent, 0)
+
+    def finish(pair, carry):
+        for side in range(2):
+            for way in ORDER:
+                fin_copy(side, pair, way).wait_recv()
+        where = pl.ds(pair * LANES, LANES)
+        sides = [(recv_fin[which, 0, pair], recv_fin[which, 1, pair]) for which in range(outer)]
+        for t, (real_part, imag_part) in enumerate(unfold_classes(sides)):
+            out_ref[0, where, t * LANES:(t + 1) * LANES] = real_part
+            out_ref[1, where, t * LANES:(t + 1) * LANES] = imag_part
+        return carry
+
+    lax.fori_loop(0, pairs, finish, 0)
+
+    def drain(pair, carry):
+        for side in range(2):
+            for way in ORDER:
+                fin_copy(side, pair, way).wait_send()
+        return carry
+
+    lax.fori_loop(0, pairs, drain, 0)
 
 
 def fast_body(wave_field, contrast, layer_of_plane, toeplitz_table, hankel_table, layer_rates):
     _, planes, rows, width_y = wave_field.shape
     lat_count, lay_count = lax.axis_size("lat"), lax.axis_size("lay")
-    device_count = lat_count * lay_count
+    outer, peers = lat_count // 2, 2 * lay_count
     width_x = rows * lat_count
-    depth = width_y // (2 * device_count)
+    depth = width_y // (2 * outer * peers)
     plane_total = planes * lay_count
     layer_count = layer_rates.shape[0]
     lines = planes * rows
-    fh, fl, ih, il, twiddle = (jnp.asarray(t) for t in split_tables(width_y))
+    pairs = planes // 2
+    fh, fl, ih, il, twiddle = (jnp.asarray(t) for t in split_tables(width_x))
+    tables = jnp.asarray(class_tables(width_y, 2 * outer))
     smem = pl.BlockSpec(memory_space=pltpu.SMEM)
     vmem = pl.BlockSpec(memory_space=pltpu.VMEM)
-    anywhere = pl.BlockSpec(memory_space=pl.ANY)
-    exchanged = (device_count, 2, 2, depth, lines)
+    far = pl.BlockSpec(memory_space=pltpu.HBM)
+    folded = (outer, 2, lines, LANES)
+    final = (outer, 2, pairs, LANES, LANES)
     tile_all = (2, plane_total, depth, width_x)
-    lays_step = 2 if lay_count % 2 == 0 else 1
+    dma = pltpu.SemaphoreType.DMA
     space = pl.pallas_call(
         functools.partial(couple_kernel, lat_count, lay_count, planes, rows),
         out_shape=jax.ShapeDtypeStruct((2, lines, width_y), jnp.float32),
-        in_specs=[smem] * 4 + [anywhere] * 5 + [vmem],
-        out_specs=anywhere,
+        in_specs=[smem] * 4 + [far] * 6 + [vmem],
+        out_specs=vmem,
         scratch_shapes=[
-            pltpu.VMEM(exchanged, jnp.float32),
-            pltpu.VMEM(exchanged, jnp.float32),
-            pltpu.VMEM(exchanged, jnp.float32),
-            pltpu.VMEM(exchanged, jnp.float32),
+            pltpu.VMEM(folded, jnp.float32),
+            pltpu.VMEM(folded, jnp.float32),
+            pltpu.VMEM((peers, outer, 2, 2, depth, lines), jnp.float32),
+            pltpu.VMEM((outer, peers, 2, 2, depth, lines), jnp.float32),
+            pltpu.VMEM((peers, 2, pairs, 2, depth, outer * LANES), jnp.float32),
+            pltpu.VMEM((peers, 2, pairs, 2, depth, outer * LANES), jnp.float32),
+            pltpu.VMEM(final, jnp.float32),
+            pltpu.VMEM(final, jnp.float32),
             pltpu.VMEM(tile_all, jnp.float32),
             pltpu.VMEM(tile_all, jnp.float32),
-            pltpu.VMEM((2, planes * lays_step, depth, width_x), jnp.float32),
+            pltpu.VMEM((2, 2 * lay_count, depth, width_x), jnp.float32),
             pltpu.VMEM((2, layer_count, 2 * plane_total - 1, depth, width_x), jnp.float32),
-            pltpu.VMEM((2, lines, width_y // 2), jnp.float32),
             pltpu.VMEM((2, lines, width_y), jnp.float32),
             pltpu.VMEM(fh.shape, fh.dtype),
             pltpu.VMEM(fl.shape, fl.dtype),
             pltpu.VMEM(ih.shape, ih.dtype),
             pltpu.VMEM(il.shape, il.dtype),
-            pltpu.VMEM((2, lines, width_y), jnp.float32),
-            pltpu.SemaphoreType.DMA((4, device_count)),
-            pltpu.SemaphoreType.DMA((4, device_count)),
-            pltpu.SemaphoreType.DMA((lines // min(lines, 2 * LANES) + 4,)),
-            pltpu.SemaphoreType.DMA((lines // LANES,)),
+            pltpu.VMEM((2,) + tables.shape[2:], tables.dtype),
+            dma((2, outer)), dma((2, outer)),
+            dma((outer, 2, peers)), dma((outer, 2, peers)),
+            dma((2, pairs, peers)), dma((2, pairs, peers)),
+            dma((2, pairs, outer)), dma((2, pairs, outer)),
+            dma((lines // LANES + 6,)),
         ],
         compiler_params=pltpu.CompilerParams(
-            collective_id=0, has_side_effects=True, vmem_limit_bytes=60 * 1024 * 1024
+            collective_id=0, has_side_effects=True, vmem_limit_bytes=48 * 1024 * 1024
         ),
         name="couple",
     )(
         layer_of_plane, layer_rates, toeplitz_table, hankel_table,
-        wave_field.reshape(2, lines, width_y), fh, fl, ih, il, twiddle,
+        wave_field.reshape(2, lines, width_y), fh, fl, ih, il, tables, twiddle,
     )
     return space.reshape(wave_field.shape) * contrast[None]
 
@@ -532,16 +684,17 @@
 def body(wave_field, *others):
     _, planes, rows, width_y = wave_field.shape
     lat_count, lay_count = lax.axis_size("lat"), lax.axis_size("lay")
-    device_count = lat_count * lay_count
+    outer, peers = lat_count // 2, 2 * lay_count
     width_x = rows * lat_count
     fits = (
-        2 * rows == LANES
+        lat_count % 2 == 0
+        and outer == 4
+        and 2 * rows == LANES
         and planes % 2 == 0
+        and planes >= 4
         and width_x == width_y
-        and width_y % (4 * LANES) == 0
-        and width_y == 2 * device_count * SUBLANES
-        and device_count % 2 == 0
-        and lat_count % 2 == 0
+        and width_y == outer * LANES
+        and width_y == 2 * outer * peers * SUBLANES
         and (planes * lay_count) % (LANES // SUBLANES) == 0
         and (planes * rows) % (2 * LANES) == 0
     )

time: 108 us -> 123 us (1.14)
  local copies, waits for them, and re-layouts: 0.01 us -> 8.78 us
  Pallas kernels: 105 us -> 112 us
  other arithmetic: 3.33 us -> 1.7 us
    unnamed x2 -> x22, local copies, waits for them, and re-layouts: 0.01 us -> 8.78 us
    pallas_call x1, Pallas kernels: 105 us -> 112 us  [fast_body(): pl.pallas_call(functools.partial(couple_kernel, lat_count, lay_count, pla...]
    mul x1, other arithmetic: 3.33 us -> 1.7 us  [fast_body(): return space.reshape(wave_field.shape) * contrast[None]]
where the time goes in v1:
time: 123 us
  Pallas kernels  112 us (91%)
  local copies, waits for them, and re-layouts  8.78 us (7%)
  other arithmetic  1.7 us (1%)
    pallas_call x1, Pallas kernels, fast_body(): pl.pallas_call(functools.partial(couple_kernel, lat_count, lay_count, pla...  112 us
    unnamed x22, local copies, waits for them, and re-layouts  8.78 us

profile of v1, /device:TPU:0, one launch (start us, length us, event | category | flops | bytes accessed | tf_op | source)
XLA Modules:
  0.0 122.9 jit_solution(9158345387953448689)
XLA Ops:
  0.0 0.0 copy-start
  0.0 1.2 copy-done
  1.2 0.0 copy-start.1
  1.2 1.0 copy-done.1
  2.3 0.0 copy-start.2
  2.3 1.0 copy-done.2
  3.3 0.0 copy-start.3
  3.3 1.0 copy-done.3
  4.4 0.0 copy-start.4
  4.4 1.0 copy-done.4
  5.4 0.0 copy-start.5
  5.4 0.7 copy-done.5
  6.1 0.0 copy-start.6
  6.1 0.7 copy-done.6
  6.8 0.0 copy-start.7
  6.8 0.7 copy-done.7
  7.5 0.0 copy-start.8
  7.5 0.7 copy-done.8
  8.1 0.0 copy-start.9
  8.1 0.7 copy-done.9
  8.8 0.0 copy-start.10
  8.8 112.4 %couple.1 = f32[2,512,512]{2,1,0:T(8,128)S(1)} custom-call(s32[32]{0:T(128)S(1)} %copy-done.8, f32[8]{0:T(128)S(1)} %copy-done.9, f32[2,8,63]{2,1,0:T(8,128)S(1)} %copy-done.5, f32[2,8,63]{2,1,0:T(8,128)S(1)} %copy-done.6, f32[2,512,512]{2,1,0:T(8,128)} %bitcast.3, bf16[512,512]{1,0:T(8,128)(2,1)S(1)} %copy-done.4, bf16[512,512]{1,0:T(8,128)(2,1)S(1)} %copy-done.3, ...), custom_call_target="tpu_custom_call" | custom-call | tf_op jit(solution)/shard_map/couple/pallas_call | solution.py:643
  121.1 0.0 copy-done.10
  121.2 1.7 %broadcast_multiply_fusion = f32[2,8,64,512]{3,2,1,0:T(8,128)} fusion(f32[2,8,64,512]{3,2,1,0:T(8,128)S(1)} %bitcast.2, f32[8,64,512]{2,1,0:T(8,128)S(1)} %copy-done.10), kind=kLoop, calls=%fused_computation | loop fusion | flops 524288 | bytes 5242880 | tf_op jit(solution)/shard_map/mul | solution.py:681
Async XLA Ops:
  0.0 1.2 copy-start
  1.2 1.0 copy-start.1
  2.3 1.0 copy-start.2
  3.3 1.0 copy-start.3
  4.4 1.0 copy-start.4
  5.4 0.7 copy-start.5
  6.1 0.7 copy-start.6
  6.8 0.7 copy-start.7
  7.5 0.7 copy-start.8
  8.1 0.7 copy-start.9
  8.8 112.4 %copy-start.10 = (f32[8,64,512]{2,1,0:T(8,128)S(1)}, f32[8,64,512]{2,1,0:T(8,128)}, u32[]{:S(2)}) copy-start(f32[8,64,512]{2,1,0:T(8,128)} %param.13) | copy-start | bytes 3145732

commit v2 on v1

--- a/solution.py
+++ b/solution.py
@@ -269,17 +269,19 @@
 
 
 ORDER = (3, 2, 1)
+PARTS = 2
 
 
 def couple_kernel(
     lat_count, lay_count, planes, rows,
-    layer_ref, rate_ref, toeplitz_ref, hankel_ref,
-    field_any, fh_any, fl_any, ih_any, il_any, tables_any, twiddle_ref,
-    out_ref,
+    layer_any, rate_any, toeplitz_any, hankel_any,
+    field_any, fh_any, fl_any, ih_any, il_any, tables_any, twiddle_any,
+    out_any,
     send_fold, recv_fold, send_in, recv_in, send_out, recv_mid, send_fin, recv_fin,
     field_x, spectrum, mixed, powers,
-    field_ref, fh_ref, fl_ref, ih_ref, il_ref, tables_ref,
-    fold_send, fold_recv, in_send, in_recv, out_send, out_recv, fin_send, fin_recv, load_sem,
+    field_ref, fh_ref, fl_ref, ih_ref, il_ref, tables_ref, twiddle_ref,
+    layer_ref, rate_ref, toeplitz_ref, hankel_ref, out_ref,
+    fold_send, fold_recv, in_send, in_recv, out_send, out_recv, fin_send, fin_recv, load_sem, store_sem,
 ):
     inner = 2
     outer = lat_count // inner
@@ -334,11 +336,14 @@
             [
                 (tables_any.at[0, my_outer], tables_ref.at[0]),
                 (tables_any.at[1, my_outer], tables_ref.at[1]),
+                (rate_any, rate_ref), (layer_any, layer_ref),
+                (toeplitz_any, toeplitz_ref), (hankel_any, hankel_ref),
                 (fh_any, fh_ref), (fl_any, fl_ref), (ih_any, ih_ref), (il_any, il_ref),
+                (twiddle_any, twiddle_ref),
             ]
         )
     ]
-    for load in loads:
+    for load in loads[:chunks]:
         load.start()
 
     barrier = pltpu.get_barrier_semaphore()
@@ -350,55 +355,76 @@
         )
     )
 
-    def remote(source, target, sems, index, device):
+    def remote(source, target, sems, device):
         return pltpu.make_async_remote_copy(
             src_ref=source,
             dst_ref=target,
-            send_sem=sems[0].at[index],
-            recv_sem=sems[1].at[index],
+            send_sem=sems[0],
+            recv_sem=sems[1],
             device_id=device,
             device_id_type=MESH,
         )
 
-    def fold_copy(side, way):
+    def wait_bytes(view, sem):
+        pltpu.make_async_copy(view, view, sem).wait()
+
+    others, ways = pl.ds(0, peers - 1), pl.ds(0, outer - 1)
+
+    def fold_copy(side, way, part):
+        where = pl.ds(part * (lines // PARTS), lines // PARTS)
         return remote(
-            send_fold.at[column(way), side], recv_fold.at[my_outer, side],
-            (fold_send, fold_recv), (side, way), column_id(way),
+            send_fold.at[column(way), side, where], recv_fold.at[my_outer, side, where],
+            (fold_send, fold_recv.at[side, way]), column_id(way),
         )
 
     def in_copy(origin, side, step):
         return remote(
             send_in.at[peer(step), origin, side], recv_in.at[origin, my_peer, side],
-            (in_send, in_recv), (origin, side, step), peer_id(step),
+            (in_send, in_recv.at[origin, side]), peer_id(step),
         )
 
     def out_copy(side, pair, step):
         return remote(
             send_out.at[peer(step), side, pair], recv_mid.at[my_peer, side, pair],
-            (out_send, out_recv), (side, pair, step), peer_id(step),
+            (out_send, out_recv.at[side, pair]), peer_id(step),
         )
 
     def fin_copy(side, pair, way):
         return remote(
             send_fin.at[column(way), side, pair], recv_fin.at[my_outer, side, pair],
-            (fin_send, fin_recv), (side, pair, way), column_id(way),
-        )
-
-    for i in range(chunks):
-        where = slice(i * chunk, (i + 1) * chunk)
-        loads[i].wait()
-        parts = [
-            [field_ref[comp, where, t * LANES:(t + 1) * LANES] for t in range(outer)]
-            for comp in range(2)
-        ]
-        for which, both in enumerate(fold_classes(*parts)):
-            for side in range(2):
-                send_fold[which, side, where] = both[side]
-
-    pl.semaphore_wait(barrier, outer - 1 + peers - 1)
-    for side in range(2):
+            (fin_send, fin_recv.at[pair]), column_id(way),
+        )
+
+    middle = (my_outer + 1) // 2 % 2
+
+    def fold(part):
+        for i in range(part * chunks // PARTS, (part + 1) * chunks // PARTS):
+            where = slice(i * chunk, (i + 1) * chunk)
+            loads[i].wait()
+            parts = [
+                [field_ref[comp, where, t * LANES:(t + 1) * LANES] for t in range(outer)]
+                for comp in range(2)
+            ]
+            for which, both in enumerate(fold_classes(*parts)):
+                for side in range(2):
+                    send_fold[which, side, where] = both[side]
+
+    def send_folded(side, part):
         for way in ORDER:
-            fold_copy(side, way).start()
+            fold_copy(side, way, part).start()
+
+    for part in range(PARTS):
+        fold(part)
+        if part == 0:
+            for load in loads[chunks:]:
+                load.start()
+            pl.semaphore_wait(barrier, outer - 1 + peers - 1)
+        send_folded(0, part)
+
+    @pl.when(middle == 1)
+    def _():
+        for part in range(PARTS):
+            send_folded(1, part)
 
     loads[chunks].wait()
     loads[chunks + 1].wait()
@@ -416,6 +442,7 @@
 
     for side in range(2):
         transform_y(send_fold, my_outer, side)
+    loads[chunks + 2].wait()
 
     def signed(index, amount):
         index = jnp.where(index >= amount // 2, index - amount, index)
@@ -441,15 +468,22 @@
 
         lax.fori_loop(0, layer_count, one_layer, 0)
 
-    for i in range(chunks + 2, chunks + 6):
-        loads[i].wait()
+    for load in loads[chunks + 3:]:
+        load.wait()
 
     def gather(side, way):
-        fold_copy(side, way).wait_recv()
+        wait_bytes(recv_fold.at[column(way), side], fold_recv.at[side, way])
         transform_y(recv_fold, column(way), side)
 
-    for way in ORDER:
-        gather(0, way)
+    early, late = 3 - middle, 2 + middle
+    gather(0, early)
+    gather(0, 1)
+    gather(0, late)
+
+    @pl.when(middle == 0)
+    def _():
+        for part in range(PARTS):
+            send_folded(1, part)
 
     def load_lines(side):
         def one_lay(lay, carry):
@@ -542,20 +576,22 @@
         lax.fori_loop(0, some_planes, one_plane, 0)
 
     def invert_y(side, pair):
-        over_peers(lambda step: out_copy(side, pair, step).wait_recv())
+        wait_bytes(recv_mid.at[others, side, pair], out_recv.at[side, pair])
         stack = jnp.concatenate(
             [recv_mid[:, side, pair, comp].reshape(length, outer * LANES) for comp in range(2)], 0
         )
         result = product((tables_ref[side, 2], tables_ref[side, 3]), split(stack), ((1,), (0,)))
         for block in range(outer):
             send_fin[block, side, pair] = result[:, block * LANES:(block + 1) * LANES].T
+        recv_fin[my_outer, side, pair] = send_fin[my_outer, side, pair]
+
+    def send_final(side, pair):
         for way in ORDER:
             fin_copy(side, pair, way).start()
-        recv_fin[my_outer, side, pair] = send_fin[my_outer, side, pair]
 
     for side in range(2):
         for origin in range(outer):
-            over_peers(lambda step: in_copy(origin, side, step).wait_recv())
+            wait_bytes(recv_in.at[origin, others, side], in_recv.at[origin, side])
         load_lines(side)
         lax.fori_loop(0, plane_total // group, transform_x, 0)
 
@@ -566,59 +602,67 @@
             over_peers(lambda step: out_copy(side, pair, step).start())
             recv_mid[my_peer, side, pair] = send_out[my_peer, side, pair]
 
+            if side == 0:
+
+                @pl.when(pair == pairs - 2)
+                def _():
+                    gather(1, early)
+
+                @pl.when(pair == pairs - 1)
+                def _():
+                    gather(1, 1)
+
             @pl.when(pair >= 1)
             def _():
                 invert_y(side, pair - 1)
-
-            if side == 0:
-
-                @pl.when(pair == pairs - 2)
-                def _():
-                    gather(1, ORDER[0])
-
-                @pl.when(pair == pairs - 1)
-                def _():
-                    gather(1, ORDER[1])
+                if side == 0:
+
+                    @pl.when(middle == 1)
+                    def _():
+                        send_final(side, pair - 1)
+
+                else:
+                    send_final(side, pair - 1)
 
             return carry
 
         lax.fori_loop(0, pairs, one_pair, 0)
+        if side == 0:
+            gather(1, late)
+
+            @pl.when(middle == 0)
+            def _():
+                for pair in range(pairs - 1):
+                    send_final(side, pair)
+
         invert_y(side, pairs - 1)
-        if side == 0:
-            gather(1, ORDER[2])
-
-    for side in range(2):
-        for way in ORDER:
-            fold_copy(side, way).wait_send()
-        for origin in range(outer):
-            over_peers(lambda step: in_copy(origin, side, step).wait_send())
-
-        def sent(pair, carry):
-            over_peers(lambda step: out_copy(side, pair, step).wait_send())
-            return carry
-
-        lax.fori_loop(0, pairs, sent, 0)
+        send_final(side, pairs - 1)
+
+    wait_bytes(send_fold.at[ways], fold_send)
+    wait_bytes(send_in.at[others], in_send)
+    wait_bytes(send_out.at[others], out_send)
+
+    def store(pair):
+        where = pl.ds(pair * LANES, LANES)
+        return pltpu.make_async_copy(
+            out_ref.at[:, where], out_any.at[:, where], store_sem.at[pair]
+        )
 
     def finish(pair, carry):
-        for side in range(2):
-            for way in ORDER:
-                fin_copy(side, pair, way).wait_recv()
+        wait_bytes(recv_fin.at[ways, :, pair], fin_recv.at[pair])
         where = pl.ds(pair * LANES, LANES)
         sides = [(recv_fin[which, 0, pair], recv_fin[which, 1, pair]) for which in range(outer)]
         for t, (real_part, imag_part) in enumerate(unfold_classes(sides)):
             out_ref[0, where, t * LANES:(t + 1) * LANES] = real_part
             out_ref[1, where, t * LANES:(t + 1) * LANES] = imag_part
+        store(pair).start()
         return carry
 
     lax.fori_loop(0, pairs, finish, 0)
 
-    def drain(pair, carry):
-        for side in range(2):
-            for way in ORDER:
-                fin_copy(side, pair, way).wait_send()
-        return carry
-
-    lax.fori_loop(0, pairs, drain, 0)
+    wait_bytes(send_fin.at[ways], fin_send)
+    for pair in range(pairs):
+        store(pair).wait()
 
 
 def fast_body(wave_field, contrast, layer_of_plane, toeplitz_table, hankel_table, layer_rates):
@@ -633,9 +677,10 @@
     pairs = planes // 2
     fh, fl, ih, il, twiddle = (jnp.asarray(t) for t in split_tables(width_x))
     tables = jnp.asarray(class_tables(width_y, 2 * outer))
-    smem = pl.BlockSpec(memory_space=pltpu.SMEM)
-    vmem = pl.BlockSpec(memory_space=pltpu.VMEM)
-    far = pl.BlockSpec(memory_space=pltpu.HBM)
+    operands = [
+        layer_of_plane, layer_rates, toeplitz_table, hankel_table,
+        wave_field.reshape(2, lines, width_y), fh, fl, ih, il, tables, twiddle,
+    ]
     folded = (outer, 2, lines, LANES)
     final = (outer, 2, pairs, LANES, LANES)
     tile_all = (2, plane_total, depth, width_x)
@@ -643,8 +688,8 @@
     space = pl.pallas_call(
         functools.partial(couple_kernel, lat_count, lay_count, planes, rows),
         out_shape=jax.ShapeDtypeStruct((2, lines, width_y), jnp.float32),
-        in_specs=[smem] * 4 + [far] * 6 + [vmem],
-        out_specs=vmem,
+        in_specs=[pl.BlockSpec(memory_space=pltpu.HBM)] * len(operands),
+        out_specs=pl.BlockSpec(memory_space=pl.ANY),
         scratch_shapes=[
             pltpu.VMEM(folded, jnp.float32),
             pltpu.VMEM(folded, jnp.float32),
@@ -664,20 +709,24 @@
             pltpu.VMEM(ih.shape, ih.dtype),
             pltpu.VMEM(il.shape, il.dtype),
             pltpu.VMEM((2,) + tables.shape[2:], tables.dtype),
-            dma((2, outer)), dma((2, outer)),
-            dma((outer, 2, peers)), dma((outer, 2, peers)),
-            dma((2, pairs, peers)), dma((2, pairs, peers)),
-            dma((2, pairs, outer)), dma((2, pairs, outer)),
-            dma((lines // LANES + 6,)),
+            pltpu.VMEM(twiddle.shape, twiddle.dtype),
+            pltpu.SMEM(layer_of_plane.shape, layer_of_plane.dtype),
+            pltpu.SMEM(layer_rates.shape, layer_rates.dtype),
+            pltpu.SMEM(toeplitz_table.shape, toeplitz_table.dtype),
+            pltpu.SMEM(hankel_table.shape, hankel_table.dtype),
+            pltpu.VMEM((2, lines, width_y), jnp.float32),
+            dma(()), dma((2, outer)),
+            dma(()), dma((outer, 2)),
+            dma(()), dma((2, pairs)),
+            dma(()), dma((pairs,)),
+            dma((lines // LANES + 11,)),
+            dma((pairs,)),
         ],
         compiler_params=pltpu.CompilerParams(
             collective_id=0, has_side_effects=True, vmem_limit_bytes=48 * 1024 * 1024
         ),
         name="couple",
-    )(
-        layer_of_plane, layer_rates, toeplitz_table, hankel_table,
-        wave_field.reshape(2, lines, width_y), fh, fl, ih, il, tables, twiddle,
-    )
+    )(*(pltpu.with_memory_space_constraint(value, pltpu.HBM) for value in operands))
     return space.reshape(wave_field.shape) * contrast[None]
 
 
@@ -696,7 +745,7 @@
         and width_y == outer * LANES
         and width_y == 2 * outer * peers * SUBLANES
         and (planes * lay_count) % (LANES // SUBLANES) == 0
-        and (planes * rows) % (2 * LANES) == 0
+        and (planes * rows) % (2 * PARTS * LANES) == 0
     )
     return (fast_body if fits else general_body)(wave_field, *others)
 

time: 123 us -> 102 us (0.83)
  Pallas kernels: 112 us -> 101 us
  local copies, waits for them, and re-layouts: 8.78 us -> 0.01 us
    pallas_call x1, Pallas kernels: 112 us -> 101 us  [fast_body(): pl.pallas_call(functools.partial(couple_kernel, lat_count, lay_count, pla...]
    unnamed x22 -> x2, local copies, waits for them, and re-layouts: 8.78 us -> 0.01 us
where the time goes in v2:
time: 102 us
  Pallas kernels  101 us (99%)
  other arithmetic  1.74 us (2%)
    pallas_call x1, Pallas kernels, fast_body(): pl.pallas_call(functools.partial(couple_kernel, lat_count, lay_count, pla...  101 us

profile of v2, /device:TPU:0, one launch (start us, length us, event | category | flops | bytes accessed | tf_op | source)
XLA Modules:
  0.0 102.3 jit_solution(5955532387647307614)
XLA Ops:
  0.0 0.0 copy-start
  0.0 100.6 %couple.1 = f32[2,512,512]{2,1,0:T(8,128)S(1)} custom-call(s32[32]{0:T(128)} %layer_any.1, f32[8]{0:T(128)} %rate_any.1, f32[2,8,63]{2,1,0:T(8,128)} %toeplitz_any.1, f32[2,8,63]{2,1,0:T(8,128)} %hankel_any.1, f32[2,512,512]{2,1,0:T(8,128)} %bitcast.3, bf16[512,512]{1,0:T(8,128)(2,1)} %constant.12.clone.fh_any, bf16[512,512]{1,0:T(8,128)(2,1)} %constant.13.clone.fl_any, ...), custom_call_target="tpu_custom_call" | custom-call | tf_op jit(solution)/shard_map/couple/pallas_call | solution.py:688
  100.6 0.0 copy-done
  100.6 1.7 %broadcast_multiply_fusion = f32[2,8,64,512]{3,2,1,0:T(8,128)} fusion(f32[2,8,64,512]{3,2,1,0:T(8,128)S(1)} %bitcast.2, f32[8,64,512]{2,1,0:T(8,128)S(1)} %copy-done), kind=kLoop, calls=%fused_computation | loop fusion | flops 524288 | bytes 5242880 | tf_op jit(solution)/shard_map/mul | solution.py:730
Async XLA Ops:
  0.0 100.6 %copy-start = (f32[8,64,512]{2,1,0:T(8,128)S(1)}, f32[8,64,512]{2,1,0:T(8,128)}, u32[]{:S(2)}) copy-start(f32[8,64,512]{2,1,0:T(8,128)} %param.13) | copy-start | bytes 3145732

commit v3 on v2

--- a/solution.py
+++ b/solution.py
@@ -275,12 +275,12 @@
 def couple_kernel(
     lat_count, lay_count, planes, rows,
     layer_any, rate_any, toeplitz_any, hankel_any,
-    field_any, fh_any, fl_any, ih_any, il_any, tables_any, twiddle_any,
+    field_any, contrast_any, fh_any, fl_any, ih_any, il_any, tables_any, twiddle_any,
     out_any,
     send_fold, recv_fold, send_in, recv_in, send_out, recv_mid, send_fin, recv_fin,
     field_x, spectrum, mixed, powers,
     field_ref, fh_ref, fl_ref, ih_ref, il_ref, tables_ref, twiddle_ref,
-    layer_ref, rate_ref, toeplitz_ref, hankel_ref, out_ref,
+    layer_ref, rate_ref, toeplitz_ref, hankel_ref, out_ref, contrast_ref,
     fold_send, fold_recv, in_send, in_recv, out_send, out_recv, fin_send, fin_recv, load_sem, store_sem,
 ):
     inner = 2
@@ -339,7 +339,7 @@
                 (rate_any, rate_ref), (layer_any, layer_ref),
                 (toeplitz_any, toeplitz_ref), (hankel_any, hankel_ref),
                 (fh_any, fh_ref), (fl_any, fl_ref), (ih_any, ih_ref), (il_any, il_ref),
-                (twiddle_any, twiddle_ref),
+                (twiddle_any, twiddle_ref), (contrast_any, contrast_ref),
             ]
         )
     ]
@@ -409,9 +409,10 @@
                 for side in range(2):
                     send_fold[which, side, where] = both[side]
 
-    def send_folded(side, part):
-        for way in ORDER:
-            fold_copy(side, way, part).start()
+    def send_folded(side, ways, parts):
+        for part in parts:
+            for way in ways:
+                fold_copy(side, way, part).start()
 
     for part in range(PARTS):
         fold(part)
@@ -419,12 +420,12 @@
             for load in loads[chunks:]:
                 load.start()
             pl.semaphore_wait(barrier, outer - 1 + peers - 1)
-        send_folded(0, part)
+        send_folded(0, ORDER, [part])
 
     @pl.when(middle == 1)
     def _():
-        for part in range(PARTS):
-            send_folded(1, part)
+        for way in (3, 1, 2):
+            send_folded(1, [way], range(PARTS))
 
     loads[chunks].wait()
     loads[chunks + 1].wait()
@@ -482,8 +483,8 @@
 
     @pl.when(middle == 0)
     def _():
-        for part in range(PARTS):
-            send_folded(1, part)
+        for way in (1, 3, 2):
+            send_folded(1, [way], range(PARTS))
 
     def load_lines(side):
         def one_lay(lay, carry):
@@ -586,7 +587,7 @@
         recv_fin[my_outer, side, pair] = send_fin[my_outer, side, pair]
 
     def send_final(side, pair):
-        for way in ORDER:
+        for way in (early, late, 1):
             fin_copy(side, pair, way).start()
 
     for side in range(2):
@@ -599,44 +600,60 @@
             couple(side, pair)
             invert_x()
             store_lines(side, pair)
+            if side == 0:
+
+                @pl.when(pair == pairs - 1)
+                def _():
+                    gather(1, 2)
+
             over_peers(lambda step: out_copy(side, pair, step).start())
             recv_mid[my_peer, side, pair] = send_out[my_peer, side, pair]
 
             if side == 0:
 
-                @pl.when(pair == pairs - 2)
-                def _():
-                    gather(1, early)
-
-                @pl.when(pair == pairs - 1)
+                @pl.when(pair == 1)
                 def _():
                     gather(1, 1)
 
-            @pl.when(pair >= 1)
-            def _():
-                invert_y(side, pair - 1)
-                if side == 0:
+                @pl.when(pair == 2 - middle)
+                def _():
+                    gather(1, 3)
+
+                @pl.when(pair >= 2)
+                def _():
+                    invert_y(0, pair - 2)
 
                     @pl.when(middle == 1)
                     def _():
-                        send_final(side, pair - 1)
-
-                else:
-                    send_final(side, pair - 1)
+                        send_final(0, pair - 2)
+
+            else:
+
+                @pl.when(pair == 0)
+                def _():
+                    invert_y(0, pairs - 1)
+                    send_final(0, pairs - 1)
+
+                @pl.when(pair >= 1)
+                def _():
+                    invert_y(1, pair - 1)
+                    send_final(1, pair - 1)
 
             return carry
 
         lax.fori_loop(0, pairs, one_pair, 0)
         if side == 0:
-            gather(1, late)
+            invert_y(0, pairs - 2)
 
             @pl.when(middle == 0)
             def _():
-                for pair in range(pairs - 1):
-                    send_final(side, pair)
-
-        invert_y(side, pairs - 1)
-        send_final(side, pairs - 1)
+                for pair in range(pairs - 2):
+                    send_final(0, pair)
+
+            send_final(0, pairs - 2)
+        else:
+            invert_y(1, pairs - 1)
+            send_final(1, pairs - 1)
 
     wait_bytes(send_fold.at[ways], fold_send)
     wait_bytes(send_in.at[others], in_send)
@@ -653,8 +670,10 @@
         where = pl.ds(pair * LANES, LANES)
         sides = [(recv_fin[which, 0, pair], recv_fin[which, 1, pair]) for which in range(outer)]
         for t, (real_part, imag_part) in enumerate(unfold_classes(sides)):
-            out_ref[0, where, t * LANES:(t + 1) * LANES] = real_part
-            out_ref[1, where, t * LANES:(t + 1) * LANES] = imag_part
+            place = slice(t * LANES, (t + 1) * LANES)
+            scale = contrast_ref[where, place]
+            out_ref[0, where, place] = real_part * scale
+            out_ref[1, where, place] = imag_part * scale
         store(pair).start()
         return carry
 
@@ -679,7 +698,7 @@
     tables = jnp.asarray(class_tables(width_y, 2 * outer))
     operands = [
         layer_of_plane, layer_rates, toeplitz_table, hankel_table,
-        wave_field.reshape(2, lines, width_y), fh, fl, ih, il, tables, twiddle,
+        wave_field.reshape(2, lines, width_y), contrast.reshape(lines, width_y), fh, fl, ih, il, tables, twiddle,
     ]
     folded = (outer, 2, lines, LANES)
     final = (outer, 2, pairs, LANES, LANES)
@@ -715,11 +734,12 @@
             pltpu.SMEM(toeplitz_table.shape, toeplitz_table.dtype),
             pltpu.SMEM(hankel_table.shape, hankel_table.dtype),
             pltpu.VMEM((2, lines, width_y), jnp.float32),
+            pltpu.VMEM((lines, width_y), jnp.float32),
             dma(()), dma((2, outer)),
             dma(()), dma((outer, 2)),
             dma(()), dma((2, pairs)),
             dma(()), dma((pairs,)),
-            dma((lines // LANES + 11,)),
+            dma((lines // LANES + 12,)),
             dma((pairs,)),
         ],
         compiler_params=pltpu.CompilerParams(
@@ -727,7 +747,7 @@
         ),
         name="couple",
     )(*(pltpu.with_memory_space_constraint(value, pltpu.HBM) for value in operands))
-    return space.reshape(wave_field.shape) * contrast[None]
+    return space.reshape(wave_field.shape)
 
 
 def body(wave_field, *others):
@@ -745,7 +765,7 @@
         and width_y == outer * LANES
         and width_y == 2 * outer * peers * SUBLANES
         and (planes * lay_count) % (LANES // SUBLANES) == 0
-        and (planes * rows) % (2 * PARTS * LANES) == 0
+        and (planes * rows) % (PARTS * LANES) == 0
     )
     return (fast_body if fits else general_body)(wave_field, *others)
 

time: 102 us -> 99.1 us (0.972)
  Pallas kernels: 101 us -> 97.6 us
  other arithmetic: 1.74 us -> 0 us
  local copies, waits for them, and re-layouts: 0.01 us -> 1.32 us
    pallas_call x1, Pallas kernels: 101 us -> 97.6 us  [fast_body(): pl.pallas_call(functools.partial(couple_kernel, lat_count, lay_count, pla...]
    mul x1 -> x0, other arithmetic: 1.74 us -> none  [fast_body(): return space.reshape(wave_field.shape) * contrast[None]]
    unnamed x2 -> x1, local copies, waits for them, and re-layouts: 0.01 us -> 1.32 us
where the time goes in v3:
time: 99.1 us; the launch traced here: 99 us
  Pallas kernels  97.6 us (98%)
  local copies, waits for them, and re-layouts  1.32 us (1%)
    pallas_call x1, Pallas kernels, fast_body(): pl.pallas_call(functools.partial(couple_kernel, lat_count, lay_count, pla...  97.6 us

profile of v3, /device:TPU:0, one launch (start us, length us, event | category | flops | bytes accessed | tf_op | source)
XLA Modules:
  0.0 99.0 jit_solution(9858899761030518591)
XLA Ops:
  0.0 97.6 %couple.1 = f32[2,512,512]{2,1,0:T(8,128)S(1)} custom-call(s32[32]{0:T(128)} %layer_any.1, f32[8]{0:T(128)} %rate_any.1, f32[2,8,63]{2,1,0:T(8,128)} %toeplitz_any.1, f32[2,8,63]{2,1,0:T(8,128)} %hankel_any.1, f32[2,512,512]{2,1,0:T(8,128)} %bitcast.4, f32[512,512]{1,0:T(8,128)} %bitcast.5, bf16[512,512]{1,0:T(8,128)(2,1)} %constant.12.clone.fh_any, ...), custom_call_target="tpu_custom_call" | custom-call | tf_op jit(solution)/shard_map/couple/pallas_call | solution.py:707
  97.6 1.3 %copy.14 = f32[2,8,64,512]{3,2,1,0:T(8,128)} copy(f32[2,8,64,512]{3,2,1,0:T(8,128)S(1)} %bitcast.3) | data formatting | bytes 4194304

commit v4 on v3

--- a/solution.py
+++ b/solution.py
@@ -269,7 +269,6 @@
 
 
 ORDER = (3, 2, 1)
-PARTS = 2
 
 
 def couple_kernel(
@@ -281,7 +280,7 @@
     field_x, spectrum, mixed, powers,
     field_ref, fh_ref, fl_ref, ih_ref, il_ref, tables_ref, twiddle_ref,
     layer_ref, rate_ref, toeplitz_ref, hankel_ref, out_ref, contrast_ref,
-    fold_send, fold_recv, in_send, in_recv, out_send, out_recv, fin_send, fin_recv, load_sem, store_sem,
+    fold_send, fold_recv, in_send, in_recv, out_send, out_recv, fin_send, fin_recv, load_sem, store_sem, second_sem, third_sem,
 ):
     inner = 2
     outer = lat_count // inner
@@ -321,15 +320,17 @@
 
         lax.fori_loop(1, peers, one, 0)
 
-    chunk = LANES
-    chunks = lines // chunk
+    chunk = LANES // 2
+    cuts = (0, chunk, lines // 2, lines)
+    spans = list(zip(cuts[:-1], cuts[1:]))
+    chunks = len(spans)
     loads = [
         pltpu.make_async_copy(
-            field_any.at[:, pl.ds(i * chunk, chunk)],
-            field_ref.at[:, pl.ds(i * chunk, chunk)],
+            field_any.at[:, pl.ds(start, stop - start)],
+            field_ref.at[:, pl.ds(start, stop - start)],
             load_sem.at[i],
         )
-        for i in range(chunks)
+        for i, (start, stop) in enumerate(spans)
     ] + [
         pltpu.make_async_copy(source, target, load_sem.at[chunks + i])
         for i, (source, target) in enumerate(
@@ -346,14 +347,29 @@
     for load in loads[:chunks]:
         load.start()
 
-    barrier = pltpu.get_barrier_semaphore()
-    for way in range(1, outer):
-        pl.semaphore_signal(barrier, inc=1, device_id=column_id(way), device_id_type=MESH)
-    over_peers(
-        lambda step: pl.semaphore_signal(
-            barrier, inc=1, device_id=peer_id(step), device_id_type=MESH
-        )
-    )
+    middle = (my_outer + 1) // 2 % 2
+    stages = [pltpu.get_barrier_semaphore(), second_sem, third_sem]
+
+    def tell(sem):
+        bit = 1
+        while bit < peers:
+            pl.semaphore_signal(
+                sem,
+                inc=1,
+                device_id=peer_id(bit - 2 * bit * (my_peer // bit % 2) + peers),
+                device_id_type=MESH,
+            )
+            bit = 2 * bit
+        pl.semaphore_signal(sem, inc=1, device_id=column_id(1), device_id_type=MESH)
+
+        @pl.when(middle == 1)
+        def _():
+            pl.semaphore_signal(sem, inc=1, device_id=column_id(3), device_id_type=MESH)
+
+    def hear(sem):
+        pl.semaphore_wait(sem, peers.bit_length() + middle)
+
+    tell(stages[0])
 
     def remote(source, target, sems, device):
         return pltpu.make_async_remote_copy(
@@ -370,8 +386,8 @@
 
     others, ways = pl.ds(0, peers - 1), pl.ds(0, outer - 1)
 
-    def fold_copy(side, way, part):
-        where = pl.ds(part * (lines // PARTS), lines // PARTS)
+    def fold_copy(side, way, start, stop):
+        where = pl.ds(start, stop - start)
         return remote(
             send_fold.at[column(way), side, where], recv_fold.at[my_outer, side, where],
             (fold_send, fold_recv.at[side, way]), column_id(way),
@@ -389,18 +405,17 @@
             (out_send, out_recv.at[side, pair]), peer_id(step),
         )
 
-    def fin_copy(side, pair, way):
+    def fin_copy(side, pair, half, way):
+        where = pl.ds(half * chunk, chunk)
         return remote(
-            send_fin.at[column(way), side, pair], recv_fin.at[my_outer, side, pair],
-            (fin_send, fin_recv.at[pair]), column_id(way),
-        )
-
-    middle = (my_outer + 1) // 2 % 2
-
-    def fold(part):
-        for i in range(part * chunks // PARTS, (part + 1) * chunks // PARTS):
-            where = slice(i * chunk, (i + 1) * chunk)
-            loads[i].wait()
+            send_fin.at[column(way), side, pair, where],
+            recv_fin.at[my_outer, side, pair, where],
+            (fin_send, fin_recv.at[pair, half]), column_id(way),
+        )
+
+    def fold(start, stop):
+        for first in range(start, stop, chunk):
+            where = slice(first, first + chunk)
             parts = [
                 [field_ref[comp, where, t * LANES:(t + 1) * LANES] for t in range(outer)]
                 for comp in range(2)
@@ -409,23 +424,45 @@
                 for side in range(2):
                     send_fold[which, side, where] = both[side]
 
-    def send_folded(side, ways, parts):
-        for part in parts:
+    def send_folded(side, ways, some):
+        for start, stop in some:
             for way in ways:
-                fold_copy(side, way, part).start()
-
-    for part in range(PARTS):
-        fold(part)
-        if part == 0:
-            for load in loads[chunks:]:
-                load.start()
-            pl.semaphore_wait(barrier, outer - 1 + peers - 1)
-        send_folded(0, ORDER, [part])
-
-    @pl.when(middle == 1)
-    def _():
-        for way in (3, 1, 2):
-            send_folded(1, [way], range(PARTS))
+                fold_copy(side, way, start, stop).start()
+
+    halves = [(0, lines // 2), (lines // 2, lines)]
+
+    def of_both(inside, outside):
+        for flag, sends in ((1, inside), (0, outside)):
+            if sends:
+
+                @pl.when(middle == flag)
+                def _():
+                    for side, way, some in sends:
+                        send_folded(side, [way], some)
+
+    def fold_next(i):
+        loads[i].wait()
+        fold(*spans[i])
+
+    fold_next(0)
+    hear(stages[0])
+    tell(stages[1])
+    of_both([(0, 3, spans[:1])], [(0, 1, spans[:1])])
+    for load in loads[chunks:]:
+        load.start()
+    fold_next(1)
+    of_both([(0, 3, spans[1:2])], [])
+    hear(stages[1])
+    tell(stages[2])
+    of_both([(0, 2, spans[:2])], [(0, 2, spans[:2])])
+    fold_next(2)
+    of_both(
+        [(0, 3, spans[2:]), (0, 2, spans[2:]), (0, 1, spans)]
+        + [(1, way, halves) for way in (3, 1, 2)],
+        [(0, 2, spans[2:])],
+    )
+    hear(stages[2])
+    of_both([], [(0, 3, spans), (0, 1, spans[1:])])
 
     loads[chunks].wait()
     loads[chunks + 1].wait()
@@ -484,7 +521,7 @@
     @pl.when(middle == 0)
     def _():
         for way in (1, 3, 2):
-            send_folded(1, [way], range(PARTS))
+            send_folded(1, [way], halves)
 
     def load_lines(side):
         def one_lay(lay, carry):
@@ -587,8 +624,9 @@
         recv_fin[my_outer, side, pair] = send_fin[my_outer, side, pair]
 
     def send_final(side, pair):
-        for way in (early, late, 1):
-            fin_copy(side, pair, way).start()
+        for half in range(2):
+            for way in (early, late, 1):
+                fin_copy(side, pair, half, way).start()
 
     for side in range(2):
         for origin in range(outer):
@@ -659,29 +697,26 @@
     wait_bytes(send_in.at[others], in_send)
     wait_bytes(send_out.at[others], out_send)
 
-    def store(pair):
-        where = pl.ds(pair * LANES, LANES)
-        return pltpu.make_async_copy(
-            out_ref.at[:, where], out_any.at[:, where], store_sem.at[pair]
-        )
-
-    def finish(pair, carry):
-        wait_bytes(recv_fin.at[ways, :, pair], fin_recv.at[pair])
-        where = pl.ds(pair * LANES, LANES)
-        sides = [(recv_fin[which, 0, pair], recv_fin[which, 1, pair]) for which in range(outer)]
+    def finish(step, carry):
+        pair, half = step // 2, step % 2
+        inside = pl.ds(half * chunk, chunk)
+        wait_bytes(recv_fin.at[ways, :, pair, inside], fin_recv.at[pair, half])
+        where = pl.ds(step * chunk, chunk)
+        sides = [
+            (recv_fin[which, 0, pair, inside], recv_fin[which, 1, pair, inside])
+            for which in range(outer)
+        ]
         for t, (real_part, imag_part) in enumerate(unfold_classes(sides)):
             place = slice(t * LANES, (t + 1) * LANES)
             scale = contrast_ref[where, place]
             out_ref[0, where, place] = real_part * scale
             out_ref[1, where, place] = imag_part * scale
-        store(pair).start()
+        pltpu.make_async_copy(out_ref.at[:, where], out_any.at[:, where], store_sem).start()
         return carry
 
-    lax.fori_loop(0, pairs, finish, 0)
-
+    lax.fori_loop(0, 2 * pairs, finish, 0)
     wait_bytes(send_fin.at[ways], fin_send)
-    for pair in range(pairs):
-        store(pair).wait()
+    wait_bytes(out_ref, store_sem)
 
 
 def fast_body(wave_field, contrast, layer_of_plane, toeplitz_table, hankel_table, layer_rates):
@@ -738,9 +773,11 @@
             dma(()), dma((2, outer)),
             dma(()), dma((outer, 2)),
             dma(()), dma((2, pairs)),
-            dma(()), dma((pairs,)),
-            dma((lines // LANES + 12,)),
-            dma((pairs,)),
+            dma(()), dma((pairs, 2)),
+            dma((15,)),
+            dma(()),
+            pltpu.SemaphoreType.REGULAR,
+            pltpu.SemaphoreType.REGULAR,
         ],
         compiler_params=pltpu.CompilerParams(
             collective_id=0, has_side_effects=True, vmem_limit_bytes=48 * 1024 * 1024
@@ -765,7 +802,7 @@
         and width_y == outer * LANES
         and width_y == 2 * outer * peers * SUBLANES
         and (planes * lay_count) % (LANES // SUBLANES) == 0
-        and (planes * rows) % (PARTS * LANES) == 0
+        and (planes * rows) % (2 * LANES) == 0
     )
     return (fast_body if fits else general_body)(wave_field, *others)
 

time: 99.1 us -> 98.4 us (level)
  no operation moved by 1% of the time
where the time goes in v4:
time: 98.4 us; the launch traced here: 98.2 us
  Pallas kernels  96.9 us (98%)
  local copies, waits for them, and re-layouts  1.32 us (1%)
    pallas_call x1, Pallas kernels, fast_body(): pl.pallas_call(functools.partial(couple_kernel, lat_count, lay_count, pla...  96.9 us

profile of v4, /device:TPU:0, one launch (start us, length us, event | category | flops | bytes accessed | tf_op | source)
XLA Modules:
  0.0 98.2 jit_solution(273465575232055733)
XLA Ops:
  0.0 96.9 %couple.1 = f32[2,512,512]{2,1,0:T(8,128)S(1)} custom-call(s32[32]{0:T(128)} %layer_any.1, f32[8]{0:T(128)} %rate_any.1, f32[2,8,63]{2,1,0:T(8,128)} %toeplitz_any.1, f32[2,8,63]{2,1,0:T(8,128)} %hankel_any.1, f32[2,512,512]{2,1,0:T(8,128)} %bitcast.4, f32[512,512]{1,0:T(8,128)} %bitcast.5, bf16[512,512]{1,0:T(8,128)(2,1)} %constant.12.clone.fh_any, ...), custom_call_target="tpu_custom_call" | custom-call | tf_op jit(solution)/shard_map/couple/pallas_call | solution.py:742
  96.9 1.3 %copy.14 = f32[2,8,64,512]{3,2,1,0:T(8,128)} copy(f32[2,8,64,512]{3,2,1,0:T(8,128)S(1)} %bitcast.3) | data formatting | bytes 4194304

commit v5 on v4

--- a/solution.py
+++ b/solution.py
@@ -156,7 +156,7 @@
     high, low = split_pair(right)
     turn = 2.0 * np.pi / amount * index
     twiddle = np.stack([np.cos(turn), np.sin(turn)]).astype(np.float32)
-    return high, low, np.ascontiguousarray(high.T), np.ascontiguousarray(low.T), twiddle
+    return np.stack([high, low, high.T, low.T]), twiddle
 
 
 def class_tables(amount, classes):
@@ -169,7 +169,8 @@
         cos_part, sin_part = np.cos(angle), np.sin(angle)
         forward = np.block([[cos_part, sin_part], [-sin_part, cos_part]])
         every.append(np.stack([*split_pair(forward), *split_pair(forward.T)]))
-    return np.stack(every).reshape(2, classes // 2, 4, 2 * length, 2 * length)
+    every = np.stack(every).reshape(2, classes // 2, 4, 2 * length, 2 * length)
+    return np.ascontiguousarray(every.swapaxes(0, 1))
 
 
 def split(value):
@@ -274,13 +275,13 @@
 def couple_kernel(
     lat_count, lay_count, planes, rows,
     layer_any, rate_any, toeplitz_any, hankel_any,
-    field_any, contrast_any, fh_any, fl_any, ih_any, il_any, tables_any, twiddle_any,
-    out_any,
+    field_any, contrast_any, lines_any, tables_any, twiddle_any,
+    out_ref,
     send_fold, recv_fold, send_in, recv_in, send_out, recv_mid, send_fin, recv_fin,
     field_x, spectrum, mixed, powers,
-    field_ref, fh_ref, fl_ref, ih_ref, il_ref, tables_ref, twiddle_ref,
-    layer_ref, rate_ref, toeplitz_ref, hankel_ref, out_ref, contrast_ref,
-    fold_send, fold_recv, in_send, in_recv, out_send, out_recv, fin_send, fin_recv, load_sem, store_sem, second_sem, third_sem,
+    field_ref, lines_ref, tables_ref, twiddle_ref,
+    layer_ref, rate_ref, toeplitz_ref, hankel_ref, contrast_ref,
+    fold_send, fold_recv, in_send, in_recv, out_send, out_recv, fin_send, fin_recv, load_sem, second_sem, third_sem,
 ):
     inner = 2
     outer = lat_count // inner
@@ -321,7 +322,7 @@
         lax.fori_loop(1, peers, one, 0)
 
     chunk = LANES // 2
-    cuts = (0, chunk, lines // 2, lines)
+    cuts = (0, 2 * chunk, lines // 2, lines)
     spans = list(zip(cuts[:-1], cuts[1:]))
     chunks = len(spans)
     loads = [
@@ -335,18 +336,13 @@
         pltpu.make_async_copy(source, target, load_sem.at[chunks + i])
         for i, (source, target) in enumerate(
             [
-                (tables_any.at[0, my_outer], tables_ref.at[0]),
-                (tables_any.at[1, my_outer], tables_ref.at[1]),
+                (tables_any.at[my_outer], tables_ref),
                 (rate_any, rate_ref), (layer_any, layer_ref),
                 (toeplitz_any, toeplitz_ref), (hankel_any, hankel_ref),
-                (fh_any, fh_ref), (fl_any, fl_ref), (ih_any, ih_ref), (il_any, il_ref),
-                (twiddle_any, twiddle_ref), (contrast_any, contrast_ref),
+                (lines_any, lines_ref), (twiddle_any, twiddle_ref), (contrast_any, contrast_ref),
             ]
         )
     ]
-    for load in loads[:chunks]:
-        load.start()
-
     middle = (my_outer + 1) // 2 % 2
     stages = [pltpu.get_barrier_semaphore(), second_sem, third_sem]
 
@@ -370,6 +366,8 @@
         pl.semaphore_wait(sem, peers.bit_length() + middle)
 
     tell(stages[0])
+    for load in loads[:chunks]:
+        load.start()
 
     def remote(source, target, sems, device):
         return pltpu.make_async_remote_copy(
@@ -390,13 +388,13 @@
         where = pl.ds(start, stop - start)
         return remote(
             send_fold.at[column(way), side, where], recv_fold.at[my_outer, side, where],
-            (fold_send, fold_recv.at[side, way]), column_id(way),
+            (fold_send, fold_recv.at[side, way - 1]), column_id(way),
         )
 
     def in_copy(origin, side, step):
         return remote(
             send_in.at[peer(step), origin, side], recv_in.at[origin, my_peer, side],
-            (in_send, in_recv.at[origin, side]), peer_id(step),
+            (in_send, in_recv.at[side]), peer_id(step),
         )
 
     def out_copy(side, pair, step):
@@ -405,12 +403,12 @@
             (out_send, out_recv.at[side, pair]), peer_id(step),
         )
 
-    def fin_copy(side, pair, half, way):
-        where = pl.ds(half * chunk, chunk)
+    def fin_copy(side, pair, start, stop, sem, way):
+        where = pl.ds(start, stop - start)
         return remote(
             send_fin.at[column(way), side, pair, where],
             recv_fin.at[my_outer, side, pair, where],
-            (fin_send, fin_recv.at[pair, half]), column_id(way),
+            (fin_send, sem), column_id(way),
         )
 
     def fold(start, stop):
@@ -429,7 +427,7 @@
             for way in ways:
                 fold_copy(side, way, start, stop).start()
 
-    halves = [(0, lines // 2), (lines // 2, lines)]
+    whole = [(0, lines)]
 
     def of_both(inside, outside):
         for flag, sends in ((1, inside), (0, outside)):
@@ -458,14 +456,13 @@
     fold_next(2)
     of_both(
         [(0, 3, spans[2:]), (0, 2, spans[2:]), (0, 1, spans)]
-        + [(1, way, halves) for way in (3, 1, 2)],
+        + [(1, way, whole) for way in (3, 1, 2)],
         [(0, 2, spans[2:])],
     )
     hear(stages[2])
     of_both([], [(0, 3, spans), (0, 1, spans[1:])])
 
     loads[chunks].wait()
-    loads[chunks + 1].wait()
 
     def transform_y(source, origin, side):
         for start in range(0, lines, 2 * LANES):
@@ -480,7 +477,7 @@
 
     for side in range(2):
         transform_y(send_fold, my_outer, side)
-    loads[chunks + 2].wait()
+    loads[chunks + 1].wait()
 
     def signed(index, amount):
         index = jnp.where(index >= amount // 2, index - amount, index)
@@ -506,11 +503,11 @@
 
         lax.fori_loop(0, layer_count, one_layer, 0)
 
-    for load in loads[chunks + 3:]:
+    for load in loads[chunks + 2:]:
         load.wait()
 
     def gather(side, way):
-        wait_bytes(recv_fold.at[column(way), side], fold_recv.at[side, way])
+        wait_bytes(recv_fold.at[column(way), side], fold_recv.at[side, way - 1])
         transform_y(recv_fold, column(way), side)
 
     early, late = 3 - middle, 2 + middle
@@ -521,7 +518,7 @@
     @pl.when(middle == 0)
     def _():
         for way in (1, 3, 2):
-            send_folded(1, [way], halves)
+            send_folded(1, [way], whole)
 
     def load_lines(side):
         def one_lay(lay, carry):
@@ -548,7 +545,7 @@
         )
         for half, pair in enumerate(halves):
             left = split(jnp.concatenate(pair, 1))
-            result = product(left, (fh_ref[...], fl_ref[...]), ((1,), (0,)))
+            result = product(left, (lines_ref[0], lines_ref[1]), ((1,), (0,)))
             for comp in range(2):
                 piece = result[:, comp * half_x:(comp + 1) * half_x]
                 spectrum[comp, some, :, half * half_x:(half + 1) * half_x] = piece.reshape(
@@ -568,7 +565,7 @@
                     [mixed[comp, :, :, place].reshape(flat) for comp in range(2)], 1
                 )
             )
-            result = product(left, (ih_ref[...], il_ref[...]), ((1,), (0,)))
+            result = product(left, (lines_ref[2], lines_ref[3]), ((1,), (0,)))
             halves.append((result[:, :half_x], result[:, half_x:]))
         real_part, imag_part = butterfly_out(halves[0], halves[1], twiddle_ref)
         full = (some_planes, depth, width_x)
@@ -624,13 +621,13 @@
         recv_fin[my_outer, side, pair] = send_fin[my_outer, side, pair]
 
     def send_final(side, pair):
-        for half in range(2):
-            for way in (early, late, 1):
-                fin_copy(side, pair, half, way).start()
+        for way in (early, late, 1):
+            fin_copy(side, pair, 0, LANES, fin_recv.at[side, pair], way).start()
+
+    ends = [(0, chunk, fin_recv.at[1, pairs - 1]), (chunk, LANES, fin_recv.at[2, 0])]
 
     for side in range(2):
-        for origin in range(outer):
-            wait_bytes(recv_in.at[origin, others, side], in_recv.at[origin, side])
+        wait_bytes(recv_in.at[:, others, side], in_recv.at[side])
         load_lines(side)
         lax.fori_loop(0, plane_total // group, transform_x, 0)
 
@@ -691,17 +688,17 @@
             send_final(0, pairs - 2)
         else:
             invert_y(1, pairs - 1)
-            send_final(1, pairs - 1)
+            for start, stop, sem in ends:
+                for way in (early, late, 1):
+                    fin_copy(1, pairs - 1, start, stop, sem, way).start()
 
     wait_bytes(send_fold.at[ways], fold_send)
     wait_bytes(send_in.at[others], in_send)
     wait_bytes(send_out.at[others], out_send)
 
-    def finish(step, carry):
-        pair, half = step // 2, step % 2
-        inside = pl.ds(half * chunk, chunk)
-        wait_bytes(recv_fin.at[ways, :, pair, inside], fin_recv.at[pair, half])
-        where = pl.ds(step * chunk, chunk)
+    def finish(pair, start, stop):
+        inside = pl.ds(start, stop - start)
+        where = pl.ds(pair * LANES + start, stop - start)
         sides = [
             (recv_fin[which, 0, pair, inside], recv_fin[which, 1, pair, inside])
             for which in range(outer)
@@ -711,12 +708,20 @@
             scale = contrast_ref[where, place]
             out_ref[0, where, place] = real_part * scale
             out_ref[1, where, place] = imag_part * scale
-        pltpu.make_async_copy(out_ref.at[:, where], out_any.at[:, where], store_sem).start()
+
+    def finish_pair(pair, carry):
+        for side in range(2):
+            wait_bytes(recv_fin.at[ways, side, pair], fin_recv.at[side, pair])
+        for start in range(0, LANES, chunk):
+            finish(pair, start, start + chunk)
         return carry
 
-    lax.fori_loop(0, 2 * pairs, finish, 0)
+    lax.fori_loop(0, pairs - 1, finish_pair, 0)
+    wait_bytes(recv_fin.at[ways, 0, pairs - 1], fin_recv.at[0, pairs - 1])
+    for start, stop, sem in ends:
+        wait_bytes(recv_fin.at[ways, 1, pairs - 1, pl.ds(start, stop - start)], sem)
+        finish(pairs - 1, start, stop)
     wait_bytes(send_fin.at[ways], fin_send)
-    wait_bytes(out_ref, store_sem)
 
 
 def fast_body(wave_field, contrast, layer_of_plane, toeplitz_table, hankel_table, layer_rates):
@@ -729,11 +734,11 @@
     layer_count = layer_rates.shape[0]
     lines = planes * rows
     pairs = planes // 2
-    fh, fl, ih, il, twiddle = (jnp.asarray(t) for t in split_tables(width_x))
+    line_tables, twiddle = (jnp.asarray(t) for t in split_tables(width_x))
     tables = jnp.asarray(class_tables(width_y, 2 * outer))
     operands = [
         layer_of_plane, layer_rates, toeplitz_table, hankel_table,
-        wave_field.reshape(2, lines, width_y), contrast.reshape(lines, width_y), fh, fl, ih, il, tables, twiddle,
+        wave_field.reshape(2, lines, width_y), contrast.reshape(lines, width_y), line_tables, tables, twiddle,
     ]
     folded = (outer, 2, lines, LANES)
     final = (outer, 2, pairs, LANES, LANES)
@@ -743,7 +748,7 @@
         functools.partial(couple_kernel, lat_count, lay_count, planes, rows),
         out_shape=jax.ShapeDtypeStruct((2, lines, width_y), jnp.float32),
         in_specs=[pl.BlockSpec(memory_space=pltpu.HBM)] * len(operands),
-        out_specs=pl.BlockSpec(memory_space=pl.ANY),
+        out_specs=pl.BlockSpec(memory_space=pltpu.VMEM),
         scratch_shapes=[
             pltpu.VMEM(folded, jnp.float32),
             pltpu.VMEM(folded, jnp.float32),
@@ -758,24 +763,19 @@
             pltpu.VMEM((2, 2 * lay_count, depth, width_x), jnp.float32),
             pltpu.VMEM((2, layer_count, 2 * plane_total - 1, depth, width_x), jnp.float32),
             pltpu.VMEM((2, lines, width_y), jnp.float32),
-            pltpu.VMEM(fh.shape, fh.dtype),
-            pltpu.VMEM(fl.shape, fl.dtype),
-            pltpu.VMEM(ih.shape, ih.dtype),
-            pltpu.VMEM(il.shape, il.dtype),
-            pltpu.VMEM((2,) + tables.shape[2:], tables.dtype),
+            pltpu.VMEM(line_tables.shape, line_tables.dtype),
+            pltpu.VMEM(tables.shape[1:], tables.dtype),
             pltpu.VMEM(twiddle.shape, twiddle.dtype),
             pltpu.SMEM(layer_of_plane.shape, layer_of_plane.dtype),
             pltpu.SMEM(layer_rates.shape, layer_rates.dtype),
             pltpu.SMEM(toeplitz_table.shape, toeplitz_table.dtype),
             pltpu.SMEM(hankel_table.shape, hankel_table.dtype),
-            pltpu.VMEM((2, lines, width_y), jnp.float32),
             pltpu.VMEM((lines, width_y), jnp.float32),
-            dma(()), dma((2, outer)),
-            dma(()), dma((outer, 2)),
+            dma(()), dma((2, outer - 1)),
+            dma(()), dma((2,)),
             dma(()), dma((2, pairs)),
-            dma(()), dma((pairs, 2)),
-            dma((15,)),
-            dma(()),
+            dma(()), dma((3, pairs)),
+            dma((11,)),
             pltpu.SemaphoreType.REGULAR,
             pltpu.SemaphoreType.REGULAR,
         ],

time: 98.4 us -> 98 us (level)
  no operation moved by 1% of the time
where the time goes in v5:
time: 98 us; the launch traced here: 97.8 us
  Pallas kernels  96.5 us (98%)
  local copies, waits for them, and re-layouts  1.32 us (1%)
    pallas_call x1, Pallas kernels, fast_body(): pl.pallas_call(functools.partial(couple_kernel, lat_count, lay_count, pla...  96.5 us

profile of v5, /device:TPU:0, one launch (start us, length us, event | category | flops | bytes accessed | tf_op | source)
XLA Modules:
  0.0 97.8 jit_solution(13571741398993477274)
XLA Ops:
  0.0 96.5 %couple.1 = f32[2,512,512]{2,1,0:T(8,128)S(1)} custom-call(s32[32]{0:T(128)} %layer_any.1, f32[8]{0:T(128)} %rate_any.1, f32[2,8,63]{2,1,0:T(8,128)} %toeplitz_any.1, f32[2,8,63]{2,1,0:T(8,128)} %hankel_any.1, f32[2,512,512]{2,1,0:T(8,128)} %bitcast.4, f32[512,512]{1,0:T(8,128)} %bitcast.5, bf16[4,512,512]{2,1,0:T(8,128)(2,1)} %constant.6.clone.lines_any, ...), custom_call_target="tpu_custom_call" | custom-call | tf_op jit(solution)/shard_map/couple/pallas_call | solution.py:747
  96.5 1.3 %copy.11 = f32[2,8,64,512]{3,2,1,0:T(8,128)} copy(f32[2,8,64,512]{3,2,1,0:T(8,128)S(1)} %bitcast.3) | data formatting | bytes 4194304

commit v6 on v5

--- a/solution.py
+++ b/solution.py
@@ -620,8 +620,12 @@
             send_fin[block, side, pair] = result[:, block * LANES:(block + 1) * LANES].T
         recv_fin[my_outer, side, pair] = send_fin[my_outer, side, pair]
 
-    def send_final(side, pair):
-        for way in (early, late, 1):
+    first = 3 - (my_outer + 1) % 2
+    second = 5 - first
+    holds = my_outer == outer // 2
+
+    def send_final(side, pair, some):
+        for way in some:
             fin_copy(side, pair, 0, LANES, fin_recv.at[side, pair], way).start()
 
     ends = [(0, chunk, fin_recv.at[1, pairs - 1]), (chunk, LANES, fin_recv.at[2, 0])]
@@ -660,19 +664,23 @@
 
                     @pl.when(middle == 1)
                     def _():
-                        send_final(0, pair - 2)
+                        send_final(0, pair - 2, (first, second, 1))
 
             else:
 
                 @pl.when(pair == 0)
                 def _():
                     invert_y(0, pairs - 1)
-                    send_final(0, pairs - 1)
+                    send_final(0, pairs - 1, (first, second, 1))
 
                 @pl.when(pair >= 1)
                 def _():
                     invert_y(1, pair - 1)
-                    send_final(1, pair - 1)
+                    send_final(1, pair - 1, (first, 1))
+
+                    @pl.when(jnp.logical_not(jnp.logical_and(holds, pair >= 2)))
+                    def _():
+                        send_final(1, pair - 1, (second,))
 
             return carry
 
@@ -683,14 +691,25 @@
             @pl.when(middle == 0)
             def _():
                 for pair in range(pairs - 2):
-                    send_final(0, pair)
-
-            send_final(0, pairs - 2)
+                    send_final(0, pair, (first, second, 1))
+
+            send_final(0, pairs - 2, (first, second, 1))
         else:
             invert_y(1, pairs - 1)
-            for start, stop, sem in ends:
-                for way in (early, late, 1):
+
+            def send_last(way):
+                for start, stop, sem in ends:
                     fin_copy(1, pairs - 1, start, stop, sem, way).start()
+
+            send_last(first)
+
+            @pl.when(holds)
+            def _():
+                for pair in range(1, pairs - 1):
+                    send_final(1, pair, (second,))
+
+            send_last(second)
+            send_last(1)
 
     wait_bytes(send_fold.at[ways], fold_send)
     wait_bytes(send_in.at[others], in_send)

time: 98 us -> 96.6 us (0.986)
  the two profiles are of different devices: /device:TPU:0 before, /device:TPU:9 now
where the time goes in v6:
time: 96.6 us; the launch traced here: 96.5 us
  Pallas kernels  95.1 us (98%)
  local copies, waits for them, and re-layouts  1.32 us (1%)
    pallas_call x1, Pallas kernels, fast_body(): pl.pallas_call(functools.partial(couple_kernel, lat_count, lay_count, pla...  95.1 us

profile of v6, /device:TPU:9, one launch (start us, length us, event | category | flops | bytes accessed | tf_op | source)
XLA Modules:
  0.0 96.5 jit_solution(12487853656413142085)
XLA Ops:
  0.0 95.1 %couple.1 = f32[2,512,512]{2,1,0:T(8,128)S(1)} custom-call(s32[32]{0:T(128)} %layer_any.1, f32[8]{0:T(128)} %rate_any.1, f32[2,8,63]{2,1,0:T(8,128)} %toeplitz_any.1, f32[2,8,63]{2,1,0:T(8,128)} %hankel_any.1, f32[2,512,512]{2,1,0:T(8,128)} %bitcast.4, f32[512,512]{1,0:T(8,128)} %bitcast.5, bf16[4,512,512]{2,1,0:T(8,128)(2,1)} %constant.6.clone.lines_any, ...), custom_call_target="tpu_custom_call" | custom-call | tf_op jit(solution)/shard_map/couple/pallas_call | solution.py:766
  95.1 1.3 %copy.11 = f32[2,8,64,512]{3,2,1,0:T(8,128)} copy(f32[2,8,64,512]{3,2,1,0:T(8,128)S(1)} %bitcast.3) | data formatting | bytes 4194304

commit v7 on v6

--- a/solution.py
+++ b/solution.py
@@ -645,6 +645,10 @@
                 def _():
                     gather(1, 2)
 
+                    @pl.when(middle == 0)
+                    def _():
+                        send_final(0, 0, (first, second, 1))
+
             over_peers(lambda step: out_copy(side, pair, step).start())
             recv_mid[my_peer, side, pair] = send_out[my_peer, side, pair]
 
@@ -662,7 +666,7 @@
                 def _():
                     invert_y(0, pair - 2)
 
-                    @pl.when(middle == 1)
+                    @pl.when(jnp.logical_or(middle == 1, pair == pairs - 1))
                     def _():
                         send_final(0, pair - 2, (first, second, 1))
 
@@ -687,11 +691,6 @@
         lax.fori_loop(0, pairs, one_pair, 0)
         if side == 0:
             invert_y(0, pairs - 2)
-
-            @pl.when(middle == 0)
-            def _():
-                for pair in range(pairs - 2):
-                    send_final(0, pair, (first, second, 1))
 
             send_final(0, pairs - 2, (first, second, 1))
         else:
@@ -815,8 +814,7 @@
         lat_count % 2 == 0
         and outer == 4
         and 2 * rows == LANES
-        and planes % 2 == 0
-        and planes >= 4
+        and planes == 2 * outer
         and width_x == width_y
         and width_y == outer * LANES
         and width_y == 2 * outer * peers * SUBLANES

time: 96.6 us -> 95.8 us (level)
  the two profiles are of different devices: /device:TPU:9 before, /device:TPU:0 now
where the time goes in v7:
time: 95.8 us; the launch traced here: 94.4 us
  Pallas kernels  93.1 us (97%)
  local copies, waits for them, and re-layouts  1.32 us (1%)
    pallas_call x1, Pallas kernels, fast_body(): pl.pallas_call(functools.partial(couple_kernel, lat_count, lay_count, pla...  93.1 us

profile of v7, /device:TPU:0, one launch (start us, length us, event | category | flops | bytes accessed | tf_op | source)
XLA Modules:
  0.0 94.4 jit_solution(7272452756808202103)
XLA Ops:
  0.0 93.1 %couple.1 = f32[2,512,512]{2,1,0:T(8,128)S(1)} custom-call(s32[32]{0:T(128)} %layer_any.1, f32[8]{0:T(128)} %rate_any.1, f32[2,8,63]{2,1,0:T(8,128)} %toeplitz_any.1, f32[2,8,63]{2,1,0:T(8,128)} %hankel_any.1, f32[2,512,512]{2,1,0:T(8,128)} %bitcast.4, f32[512,512]{1,0:T(8,128)} %bitcast.5, bf16[4,512,512]{2,1,0:T(8,128)(2,1)} %constant.6.clone.lines_any, ...), custom_call_target="tpu_custom_call" | custom-call | tf_op jit(solution)/shard_map/couple/pallas_call | solution.py:765
  93.1 1.3 %copy.11 = f32[2,8,64,512]{3,2,1,0:T(8,128)} copy(f32[2,8,64,512]{3,2,1,0:T(8,128)S(1)} %bitcast.3) | data formatting | bytes 4194304
